TPU v7x, 256 devices: a whole 4x4x8 slice. The times are simulated.
256 devices in a mesh: rows: 32 (over z, y), feat: 8 (over x, core).
Axes of the slice: x: 4, y: 4, z: 8, core: 2. Of those that a mesh axis runs over, the one named last changes fastest.
Arguments:
- gradient: float32 [524288], P('rows'), may hold values from -6 to 6
- hessian: bfloat16 [524288], P('rows'), may hold values from 0.049804688 to 1
- groups: int32 [524288], P('rows'), may hold values from 0 to 16383
- leaf_ids: int32 [524288], P('rows'), may hold values from 0 to 31
- bins: int32 [256, 524288], P('feat', 'rows'), may hold values from 0 to 63
- group_sizes: int32 [16384], P('rows'), may hold values from 16 to 63
- variance_ratio: float32 [1], replicated, may hold values from 1 to 16
Outputs:
- histograms: float32 [32, 256, 128], P('rows', 'feat')
- group_means: float32 [16384], P('rows')
All inputs are finite; a program needn't handle non-finite values.
Results may differ from a plain program's by a relative error of at most 0.00038.
Values sent between devices are 32-bit elements; how exact they have to be, the bound alone decides.
A program may use at most 64 MiB of HBM per device.

v0:
```python
import jax
import jax.numpy as jnp
from jax import lax
from jax.sharding import PartitionSpec as P

BINS = 64
LEAVES = 32


def split_up(x, dim, count):
    dims = x.shape
    tiles = x.reshape(*dims[:dim], count, dims[dim] // count, *dims[dim + 1 :])
    return jnp.moveaxis(tiles, dim, 0)


def sum_at_owner(x, axis, dim):
    count = lax.axis_size(axis)
    tiles = lax.all_to_all(split_up(x, dim, count), axis, 0, 0, tiled=True)
    return jnp.sum(tiles, axis=0)


def laid_out(tiles, dim):
    dims = list(tiles.shape[1:])
    dims[dim] *= tiles.shape[0]
    return jnp.moveaxis(tiles, 0, dim).reshape(dims)


def from_everyone(x, axis):
    count = lax.axis_size(axis)
    return lax.all_to_all(jnp.broadcast_to(x[None], (count, *x.shape)), axis, 0, 0, tiled=True)


def gathered_copies(x, axis, dim):
    return laid_out(from_everyone(x, axis), dim)


def hist_term(leaf_ids, weights, bin_rows, leaf_count, bins_n):
    channels = len(weights)
    feature_count, row_count = bin_rows.shape
    block_rows = min(2048, row_count)
    turn_count = row_count // block_rows
    levels = jnp.arange(bins_n, dtype=jnp.int32)
    wanted = jnp.arange(leaf_count, dtype=jnp.int32)
    stacked = jnp.stack(weights)

    def advance(turn_no, summed):
        offset = turn_no * block_rows
        leaf_block = lax.dynamic_slice_in_dim(leaf_ids, offset, block_rows, 0)
        weight_block = lax.dynamic_slice_in_dim(stacked, offset, block_rows, 1)
        bin_block = lax.dynamic_slice_in_dim(bin_rows, offset, block_rows, 1)
        member = (leaf_block[None, :] == wanted[:, None]).astype(jnp.bfloat16)
        left_side = (member[:, None, :] * weight_block[None, :, :]).reshape(
            leaf_count * channels, block_rows
        )
        right_side = (bin_block[:, None, :] == levels[None, :, None]).astype(jnp.bfloat16)
        right_side = right_side.reshape(feature_count * bins_n, block_rows)
        return summed + lax.dot_general(
            left_side, right_side, (((1,), (1,)), ((), ())), preferred_element_type=jnp.float32
        )

    initial = jnp.zeros((leaf_count * channels, feature_count * bins_n), jnp.float32)
    summed = lax.fori_loop(0, turn_count, advance, initial)
    summed = summed.reshape(leaf_count, channels, feature_count, bins_n).transpose(0, 2, 1, 3)
    return summed.reshape(leaf_count, feature_count, channels * bins_n)


def group_sum_dense(values, ids, group_count):
    high_count = group_count // 128
    row_count = values.shape[0]
    block_rows = min(2048, row_count)
    turn_count = row_count // block_rows
    high_levels = jnp.arange(high_count, dtype=jnp.int32)
    low_levels = jnp.arange(128, dtype=jnp.int32)

    def advance(turn_no, summed):
        offset = turn_no * block_rows
        id_block = lax.dynamic_slice_in_dim(ids, offset, block_rows, 0)
        value_block = lax.dynamic_slice_in_dim(values, offset, block_rows, 0)
        high_hot = (id_block[:, None] // 128 == high_levels[None, :]).astype(jnp.float32)
        low_hot = (id_block[:, None] % 128 == low_levels[None, :]).astype(
            jnp.float32
        ) * value_block[:, None]
        return summed + lax.dot_general(
            high_hot,
            low_hot,
            (((0,), (0,)), ((), ())),
            precision=lax.Precision.HIGHEST,
            preferred_element_type=jnp.float32,
        )

    initial = jnp.zeros((high_count, 128), jnp.float32)
    return lax.fori_loop(0, turn_count, advance, initial).reshape(group_count)


def group_lookup(table, ids):
    high_count = table.shape[0] // 128
    grid = table.reshape(high_count, 128)
    row_count = ids.shape[0]
    block_rows = min(2048, row_count)
    turn_count = row_count // block_rows
    high_levels = jnp.arange(high_count, dtype=jnp.int32)
    low_levels = jnp.arange(128, dtype=jnp.int32)

    def advance(turn_no, result):
        offset = turn_no * block_rows
        id_block = lax.dynamic_slice_in_dim(ids, offset, block_rows, 0)
        high_hot = (id_block[:, None] // 128 == high_levels[None, :]).astype(jnp.float32)
        picked = jnp.dot(
            high_hot, grid, precision=lax.Precision.HIGHEST, preferred_element_type=jnp.float32
        )
        low_hot = id_block[:, None] % 128 == low_levels[None, :]
        found = jnp.sum(jnp.where(low_hot, picked, 0.0), axis=1)
        return lax.dynamic_update_slice_in_dim(result, found, offset, 0)

    initial = jnp.zeros((row_count,), jnp.float32)
    return lax.fori_loop(0, turn_count, advance, initial)


def shards(gradient, hessian, groups, leaf_ids, bins, group_sizes, variance_ratio):
    owners = lax.axis_size("rows")
    own_groups = group_sizes.shape[0]
    group_count = own_groups * owners
    leaf_share = LEAVES // owners
    ratio = variance_ratio[0]
    partial_value = group_sum_dense(gradient, groups, group_count)
    totals = sum_at_owner(partial_value, "rows", 0)
    own_means = -totals / (group_sizes.astype(jnp.float32) + ratio)
    all_means = gathered_copies(own_means, "rows", 0)
    row_means = group_lookup(all_means, groups)
    adjusted = (gradient + hessian.astype(jnp.float32) * row_means).astype(jnp.bfloat16)
    histograms = sum_at_owner(
        hist_term(leaf_ids, (adjusted, hessian), bins, leaf_share * lax.axis_size("rows"), BINS),
        "rows",
        0,
    )
    return (histograms, own_means)


def solution(mesh):
    in_specs = (P("rows"), P("rows"), P("rows"), P("rows"), P("feat", "rows"), P("rows"), P())
    out_specs = (P("rows", "feat", None), P("rows"))
    return jax.shard_map(shards, mesh=mesh, in_specs=in_specs, out_specs=out_specs, check_vma=False)
```

profile of v0, /device:TPU:4, one launch (start us, length us, event | category | flops | bytes accessed | tf_op | source)
XLA Modules:
  0.0 179.8 jit_solution(4002487699497952010)
XLA Ops:
  0.7 43.0 %while.50 = (s32[]{:T(128)}, f32[128,128]{1,0:T(8,128)}, s32[16384]{0:T(1024)}, f32[16384]{0:T(1024)}, s32[]{:T(128)}, /*index=5*/s32[]{:T(128)}, s32[]{:T(128)}, s32[]{:T(128)}) while((s32[]{:T(128)}, f32[128,128]{1,0:T(8,128)}, s32[16384]{0:T(1024)}, f32[16384]{0:T(1024)}, s32[]{:T(128)}, /*index=5*/s32[]{:T(128)}, ...), condition=%wide.region_1.2_spmd.clone.clone, body=%wide.region_0.1_spmd.clone.clone.sunk | while | flops 403523584 | bytes 209057 | solution.py:92
  2.1 0.7 add_select_fusion.11
  2.8 2.5 %convolution_add_fusion.5 = f32[128,128]{1,0:T(8,128)} fusion(f32[2048]{0:T(1024)S(1)} %dynamic_slice.96, s32[2048]{0:T(1024)S(1)} %add_select_fusion.11, s32[2048]{0:T(1024)S(1)} %get-tuple-element.652, f32[128,128]{1,0:T(8,128)} %get-tuple-element.662, pred[]{:T(512)S(6)} %compare.33), kind=kOutput, calls=%fused_computation.27.clone.1 | convolution fusion | flops 403472384 | bytes 155649 | tf_op jit(solution)/shard_map/while/body/eval_jaxpr/dot_general | solution.py:83
  6.7 0.7 add_select_fusion.11
  7.4 3.4 %convolution_add_fusion.5 = f32[128,128]{1,0:T(8,128)} fusion(f32[2048]{0:T(1024)S(1)} %dynamic_slice.96, s32[2048]{0:T(1024)S(1)} %add_select_fusion.11, s32[2048]{0:T(1024)S(1)} %get-tuple-element.652, f32[128,128]{1,0:T(8,128)} %get-tuple-element.662, pred[]{:T(512)S(6)} %compare.33), kind=kOutput, calls=%fused_computation.27.clone.1 | convolution fusion | flops 403472384 | bytes 155649 | tf_op jit(solution)/shard_map/while/body/eval_jaxpr/dot_general | solution.py:83
  12.2 0.7 add_select_fusion.11
  12.9 3.4 %convolution_add_fusion.5 = f32[128,128]{1,0:T(8,128)} fusion(f32[2048]{0:T(1024)S(1)} %dynamic_slice.96, s32[2048]{0:T(1024)S(1)} %add_select_fusion.11, s32[2048]{0:T(1024)S(1)} %get-tuple-element.652, f32[128,128]{1,0:T(8,128)} %get-tuple-element.662, pred[]{:T(512)S(6)} %compare.33), kind=kOutput, calls=%fused_computation.27.clone.1 | convolution fusion | flops 403472384 | bytes 155649 | tf_op jit(solution)/shard_map/while/body/eval_jaxpr/dot_general | solution.py:83
  17.7 0.7 add_select_fusion.11
  18.4 3.4 %convolution_add_fusion.5 = f32[128,128]{1,0:T(8,128)} fusion(f32[2048]{0:T(1024)S(1)} %dynamic_slice.96, s32[2048]{0:T(1024)S(1)} %add_select_fusion.11, s32[2048]{0:T(1024)S(1)} %get-tuple-element.652, f32[128,128]{1,0:T(8,128)} %get-tuple-element.662, pred[]{:T(512)S(6)} %compare.33), kind=kOutput, calls=%fused_computation.27.clone.1 | convolution fusion | flops 403472384 | bytes 155649 | tf_op jit(solution)/shard_map/while/body/eval_jaxpr/dot_general | solution.py:83
  23.2 0.7 add_select_fusion.11
  23.9 3.4 %convolution_add_fusion.5 = f32[128,128]{1,0:T(8,128)} fusion(f32[2048]{0:T(1024)S(1)} %dynamic_slice.96, s32[2048]{0:T(1024)S(1)} %add_select_fusion.11, s32[2048]{0:T(1024)S(1)} %get-tuple-element.652, f32[128,128]{1,0:T(8,128)} %get-tuple-element.662, pred[]{:T(512)S(6)} %compare.33), kind=kOutput, calls=%fused_computation.27.clone.1 | convolution fusion | flops 403472384 | bytes 155649 | tf_op jit(solution)/shard_map/while/body/eval_jaxpr/dot_general | solution.py:83
  28.6 0.7 add_select_fusion.11
  29.4 3.4 %convolution_add_fusion.5 = f32[128,128]{1,0:T(8,128)} fusion(f32[2048]{0:T(1024)S(1)} %dynamic_slice.96, s32[2048]{0:T(1024)S(1)} %add_select_fusion.11, s32[2048]{0:T(1024)S(1)} %get-tuple-element.652, f32[128,128]{1,0:T(8,128)} %get-tuple-element.662, pred[]{:T(512)S(6)} %compare.33), kind=kOutput, calls=%fused_computation.27.clone.1 | convolution fusion | flops 403472384 | bytes 155649 | tf_op jit(solution)/shard_map/while/body/eval_jaxpr/dot_general | solution.py:83
  34.8 3.4 %convolution_add_fusion.5 = f32[128,128]{1,0:T(8,128)} fusion(f32[2048]{0:T(1024)S(1)} %dynamic_slice.96, s32[2048]{0:T(1024)S(1)} %add_select_fusion.11, s32[2048]{0:T(1024)S(1)} %get-tuple-element.652, f32[128,128]{1,0:T(8,128)} %get-tuple-element.662, pred[]{:T(512)S(6)} %compare.33), kind=kOutput, calls=%fused_computation.27.clone.1 | convolution fusion | flops 403472384 | bytes 155649 | tf_op jit(solution)/shard_map/while/body/eval_jaxpr/dot_general | solution.py:83
  39.6 0.7 add_select_fusion.11
  40.3 3.4 %convolution_add_fusion.5 = f32[128,128]{1,0:T(8,128)} fusion(f32[2048]{0:T(1024)S(1)} %dynamic_slice.96, s32[2048]{0:T(1024)S(1)} %add_select_fusion.11, s32[2048]{0:T(1024)S(1)} %get-tuple-element.652, f32[128,128]{1,0:T(8,128)} %get-tuple-element.662, pred[]{:T(512)S(6)} %compare.33), kind=kOutput, calls=%fused_computation.27.clone.1 | convolution fusion | flops 403472384 | bytes 155649 | tf_op jit(solution)/shard_map/while/body/eval_jaxpr/dot_general | solution.py:83
  43.7 11.6 %all-to-all-start = ((f32[32,1,512]{2,1,0:T(1,128)}), f32[32,1,512]{2,1,0:T(1,128)S(1)}, u32[]{:S(2)}, u32[]{:S(2)}) async-start(f32[32,1,512]{2,1,0:T(1,128)} %bitcast), calls=%async_computation | async-start | bytes 131072 | tf_op jit(solution)/shard_map/all_to_all | solution.py:18
  55.9 9.3 %all-to-all-done = f32[32,1,512]{2,1,0:T(1,128)S(1)} async-done(((f32[32,1,512]{2,1,0:T(1,128)}), f32[32,1,512]{2,1,0:T(1,128)S(1)}, u32[]{:S(2)}, u32[]{:S(2)}) %all-to-all-start) | async-done | bytes 65568 | tf_op jit(solution)/shard_map/all_to_all | solution.py:18
  66.0 3.8 %all-to-all-start.1 = ((f32[32,1,512]{2,1,0:T(1,128)}), f32[32,1,512]{2,1,0:T(1,128)S(1)}, u32[]{:S(2)}, u32[]{:S(2)}) async-start(f32[32,1,512]{2,1,0:T(1,128)} %broadcast_in_dim.62), calls=%async_computation.1 | async-start | bytes 131072 | tf_op jit(solution)/shard_map/all_to_all | solution.py:30
  69.9 10.0 %all-to-all-done.1 = f32[32,1,512]{2,1,0:T(1,128)S(1)} async-done(((f32[32,1,512]{2,1,0:T(1,128)}), f32[32,1,512]{2,1,0:T(1,128)S(1)}, u32[]{:S(2)}, u32[]{:S(2)}) %all-to-all-start.1) | async-done | bytes 65568 | tf_op jit(solution)/shard_map/all_to_all | solution.py:30
  79.9 19.6 %while.48 = (s32[]{:T(128)}, f32[16384]{0:T(1024)S(1)}, s32[16384]{0:T(1024)}, f32[128,128]{1,0:T(8,128)S(1)}, s32[]{:T(128)}, /*index=5*/s32[]{:T(128)}, s32[]{:T(128)}, s32[]{:T(128)}) while((s32[]{:T(128)}, f32[16384]{0:T(1024)S(1)}, s32[16384]{0:T(1024)}, f32[128,128]{1,0:T(8,128)S(1)}, s32[]{:T(128)}, ...), condition=%wide.region_5.6_spmd.clone.clone, body=%wide.region_3.5_spmd.clone.clone.sunk | while | flops 403750912 | bytes 143503 | solution.py:116
  99.8 58.7 %while.49 = (s32[]{:T(128)}, f32[64,2048]{1,0:T(8,128)S(1)}, s32[16384]{0:T(1024)}, bf16[2,16384]{1,0:T(2,128)(2,1)S(1)}, s32[32,16384]{1,0:T(8,128)}, /*index=5*/s32[]{:T(128)}, s32[]{:T(128)}, s32[]{:T(128)}, s32[]{:T(128)}) while((s32[]{:T(128)}, f32[64,2048]{1,0:T(8,128)S(1)}, s32[16384]{0:T(1024)}, ...), condition=%wide.region_7.8_spmd.clone, body=%wide.region_6.7_spmd.clone.sunk | while | flops 541589504 | bytes 11583657 | solution.py:62
  100.9 1.0 constant_dynamic-slice_fusion.5
  101.9 2.5 %iota_compare_fusion.13 = pred[32,64,2048]{2,1,0:T(32,128)(4,1)S(1)} fusion(s32[32,2048]{1,0:T(8,128)S(1)} %constant_dynamic-slice_fusion.5), kind=kLoop, calls=%fused_computation.18.clone.1 | loop fusion | flops 4194304 | bytes 4456448 | tf_op jit(solution)/shard_map/while/body/eval_jaxpr/eq | solution.py:55
  104.4 2.7 %convolution_add_fusion.4 = f32[64,2048]{1,0:T(8,128)S(1)} fusion(bf16[64,2048]{1,0:T(8,128)(2,1)S(1)} %mul.124, pred[2048,2048]{1,0:T(32,128)(4,1)S(1)} %bitcast.21, f32[64,2048]{1,0:T(8,128)S(1)} %get-tuple-element.711, pred[]{:T(512)S(6)} %compare.32), kind=kOutput, calls=%fused_computation.19.clone.1 | convolution fusion | flops 537133056 | bytes 5505025 | tf_op jit(solution)/shard_map/while/body/eval_jaxpr/dot_general | solution.py:57
  108.3 1.0 constant_dynamic-slice_fusion.5
  109.2 2.5 %iota_compare_fusion.13 = pred[32,64,2048]{2,1,0:T(32,128)(4,1)S(1)} fusion(s32[32,2048]{1,0:T(8,128)S(1)} %constant_dynamic-slice_fusion.5), kind=kLoop, calls=%fused_computation.18.clone.1 | loop fusion | flops 4194304 | bytes 4456448 | tf_op jit(solution)/shard_map/while/body/eval_jaxpr/eq | solution.py:55
  111.7 2.7 %convolution_add_fusion.4 = f32[64,2048]{1,0:T(8,128)S(1)} fusion(bf16[64,2048]{1,0:T(8,128)(2,1)S(1)} %mul.124, pred[2048,2048]{1,0:T(32,128)(4,1)S(1)} %bitcast.21, f32[64,2048]{1,0:T(8,128)S(1)} %get-tuple-element.711, pred[]{:T(512)S(6)} %compare.32), kind=kOutput, calls=%fused_computation.19.clone.1 | convolution fusion | flops 537133056 | bytes 5505025 | tf_op jit(solution)/shard_map/while/body/eval_jaxpr/dot_general | solution.py:57
  115.6 1.0 constant_dynamic-slice_fusion.5
  116.6 2.5 %iota_compare_fusion.13 = pred[32,64,2048]{2,1,0:T(32,128)(4,1)S(1)} fusion(s32[32,2048]{1,0:T(8,128)S(1)} %constant_dynamic-slice_fusion.5), kind=kLoop, calls=%fused_computation.18.clone.1 | loop fusion | flops 4194304 | bytes 4456448 | tf_op jit(solution)/shard_map/while/body/eval_jaxpr/eq | solution.py:55
  119.1 2.7 %convolution_add_fusion.4 = f32[64,2048]{1,0:T(8,128)S(1)} fusion(bf16[64,2048]{1,0:T(8,128)(2,1)S(1)} %mul.124, pred[2048,2048]{1,0:T(32,128)(4,1)S(1)} %bitcast.21, f32[64,2048]{1,0:T(8,128)S(1)} %get-tuple-element.711, pred[]{:T(512)S(6)} %compare.32), kind=kOutput, calls=%fused_computation.19.clone.1 | convolution fusion | flops 537133056 | bytes 5505025 | tf_op jit(solution)/shard_map/while/body/eval_jaxpr/dot_general | solution.py:57
  122.9 1.0 constant_dynamic-slice_fusion.5
  123.9 2.5 %iota_compare_fusion.13 = pred[32,64,2048]{2,1,0:T(32,128)(4,1)S(1)} fusion(s32[32,2048]{1,0:T(8,128)S(1)} %constant_dynamic-slice_fusion.5), kind=kLoop, calls=%fused_computation.18.clone.1 | loop fusion | flops 4194304 | bytes 4456448 | tf_op jit(solution)/shard_map/while/body/eval_jaxpr/eq | solution.py:55
  126.4 2.7 %convolution_add_fusion.4 = f32[64,2048]{1,0:T(8,128)S(1)} fusion(bf16[64,2048]{1,0:T(8,128)(2,1)S(1)} %mul.124, pred[2048,2048]{1,0:T(32,128)(4,1)S(1)} %bitcast.21, f32[64,2048]{1,0:T(8,128)S(1)} %get-tuple-element.711, pred[]{:T(512)S(6)} %compare.32), kind=kOutput, calls=%fused_computation.19.clone.1 | convolution fusion | flops 537133056 | bytes 5505025 | tf_op jit(solution)/shard_map/while/body/eval_jaxpr/dot_general | solution.py:57
  130.3 1.0 constant_dynamic-slice_fusion.5
  131.3 2.5 %iota_compare_fusion.13 = pred[32,64,2048]{2,1,0:T(32,128)(4,1)S(1)} fusion(s32[32,2048]{1,0:T(8,128)S(1)} %constant_dynamic-slice_fusion.5), kind=kLoop, calls=%fused_computation.18.clone.1 | loop fusion | flops 4194304 | bytes 4456448 | tf_op jit(solution)/shard_map/while/body/eval_jaxpr/eq | solution.py:55
  133.7 2.7 %convolution_add_fusion.4 = f32[64,2048]{1,0:T(8,128)S(1)} fusion(bf16[64,2048]{1,0:T(8,128)(2,1)S(1)} %mul.124, pred[2048,2048]{1,0:T(32,128)(4,1)S(1)} %bitcast.21, f32[64,2048]{1,0:T(8,128)S(1)} %get-tuple-element.711, pred[]{:T(512)S(6)} %compare.32), kind=kOutput, calls=%fused_computation.19.clone.1 | convolution fusion | flops 537133056 | bytes 5505025 | tf_op jit(solution)/shard_map/while/body/eval_jaxpr/dot_general | solution.py:57
  137.6 1.0 constant_dynamic-slice_fusion.5
  138.6 2.5 %iota_compare_fusion.13 = pred[32,64,2048]{2,1,0:T(32,128)(4,1)S(1)} fusion(s32[32,2048]{1,0:T(8,128)S(1)} %constant_dynamic-slice_fusion.5), kind=kLoop, calls=%fused_computation.18.clone.1 | loop fusion | flops 4194304 | bytes 4456448 | tf_op jit(solution)/shard_map/while/body/eval_jaxpr/eq | solution.py:55
  141.1 2.7 %convolution_add_fusion.4 = f32[64,2048]{1,0:T(8,128)S(1)} fusion(bf16[64,2048]{1,0:T(8,128)(2,1)S(1)} %mul.124, pred[2048,2048]{1,0:T(32,128)(4,1)S(1)} %bitcast.21, f32[64,2048]{1,0:T(8,128)S(1)} %get-tuple-element.711, pred[]{:T(512)S(6)} %compare.32), kind=kOutput, calls=%fused_computation.19.clone.1 | convolution fusion | flops 537133056 | bytes 5505025 | tf_op jit(solution)/shard_map/while/body/eval_jaxpr/dot_general | solution.py:57
  145.0 1.0 constant_dynamic-slice_fusion.5
  145.9 2.5 %iota_compare_fusion.13 = pred[32,64,2048]{2,1,0:T(32,128)(4,1)S(1)} fusion(s32[32,2048]{1,0:T(8,128)S(1)} %constant_dynamic-slice_fusion.5), kind=kLoop, calls=%fused_computation.18.clone.1 | loop fusion | flops 4194304 | bytes 4456448 | tf_op jit(solution)/shard_map/while/body/eval_jaxpr/eq | solution.py:55
  148.4 2.7 %convolution_add_fusion.4 = f32[64,2048]{1,0:T(8,128)S(1)} fusion(bf16[64,2048]{1,0:T(8,128)(2,1)S(1)} %mul.124, pred[2048,2048]{1,0:T(32,128)(4,1)S(1)} %bitcast.21, f32[64,2048]{1,0:T(8,128)S(1)} %get-tuple-element.711, pred[]{:T(512)S(6)} %compare.32), kind=kOutput, calls=%fused_computation.19.clone.1 | convolution fusion | flops 537133056 | bytes 5505025 | tf_op jit(solution)/shard_map/while/body/eval_jaxpr/dot_general | solution.py:57
  152.3 1.0 constant_dynamic-slice_fusion.5
  153.3 2.5 %iota_compare_fusion.13 = pred[32,64,2048]{2,1,0:T(32,128)(4,1)S(1)} fusion(s32[32,2048]{1,0:T(8,128)S(1)} %constant_dynamic-slice_fusion.5), kind=kLoop, calls=%fused_computation.18.clone.1 | loop fusion | flops 4194304 | bytes 4456448 | tf_op jit(solution)/shard_map/while/body/eval_jaxpr/eq | solution.py:55
  155.8 2.7 %convolution_add_fusion.4 = f32[64,2048]{1,0:T(8,128)S(1)} fusion(bf16[64,2048]{1,0:T(8,128)(2,1)S(1)} %mul.124, pred[2048,2048]{1,0:T(32,128)(4,1)S(1)} %bitcast.21, f32[64,2048]{1,0:T(8,128)S(1)} %get-tuple-element.711, pred[]{:T(512)S(6)} %compare.32), kind=kOutput, calls=%fused_computation.19.clone.1 | convolution fusion | flops 537133056 | bytes 5505025 | tf_op jit(solution)/shard_map/while/body/eval_jaxpr/dot_general | solution.py:57
  158.9 0.8 copy.13
  160.3 18.8 %all_to_all.20 = f32[32,1,32,128]{3,2,1,0:T(8,128)S(1)} all-to-all(f32[32,1,32,128]{3,2,1,0:T(8,128)S(1)} %bitcast.23), channel_id=1, replica_groups=mesh['rows'=32,'feat'=8] {'rows'}, dimensions={0} | all-to-all | bytes 1048576 | tf_op jit(solution)/shard_map/all_to_all | solution.py:18
  (110 shorter events, 43.1 us)
Async XLA Ops:
  0.6 64.7 %copy-start.3 = (s32[512]{0:T(512)S(1)}, s32[512]{0:T(512)}, u32[]{:S(2)}) copy-start(s32[512]{0:T(512)} %param.18) | copy-start | bytes 6148
  0.6 69.2 %copy-start.1 = (bf16[16384]{0:T(1024)(128)(2,1)S(1)}, bf16[16384]{0:T(1024)(128)(2,1)}, u32[]{:S(2)}) copy-start(bf16[16384]{0:T(1024)(128)(2,1)} %param.14) | copy-start | bytes 98308
  43.7 55.9 %copy-start = (f32[16384]{0:T(1024)S(1)}, f32[16384]{0:T(1024)}, u32[]{:S(2)}) copy-start(f32[16384]{0:T(1024)} %get-tuple-element.730) | copy-start | bytes 196612
  43.7 21.6 %all-to-all-start = ((f32[32,1,512]{2,1,0:T(1,128)}), f32[32,1,512]{2,1,0:T(1,128)S(1)}, u32[]{:S(2)}, u32[]{:S(2)}) async-start(f32[32,1,512]{2,1,0:T(1,128)} %bitcast), calls=%async_computation | async-start | bytes 131072 | tf_op jit(solution)/shard_map/all_to_all | solution.py:18
  65.4 34.4 %copy-start.2 = (f32[512]{0:T(512)}, f32[512]{0:T(512)S(1)}, u32[]{:S(2)}) copy-start(f32[512]{0:T(512)S(1)} %add_divide_fusion) | copy-start | bytes 6148
  66.0 13.9 %all-to-all-start.1 = ((f32[32,1,512]{2,1,0:T(1,128)}), f32[32,1,512]{2,1,0:T(1,128)S(1)}, u32[]{:S(2)}, u32[]{:S(2)}) async-start(f32[32,1,512]{2,1,0:T(1,128)} %broadcast_in_dim.62), calls=%async_computation.1 | async-start | bytes 131072 | tf_op jit(solution)/shard_map/all_to_all | solution.py:30
where the time goes:
time: 183 us; the launch traced here: 180 us
  matrix products  53.2 us (29%)
  other arithmetic  45.8 us (25%)
  local copies, waits for them, and re-layouts  25.1 us (14%)
  waiting for transfers between devices  19.3 us (11%)
  blocking collectives  18.8 us (10%)
  starting transfers between devices  15.5 us (8%)
    dot_general x8, matrix products, advance(): lax.dot_general(high_hot, low_hot, (((0,), (0,)), ((), ())), precision=la...  26 us
    dot_general x8, matrix products, advance(): lax.dot_general(left_side, right_side, (((1,), (1,)), ((), ())), preferre...  21.6 us
    eq x8, other arithmetic, advance(): bin_block[:, None, :] == levels[None, :, None]  19.8 us
    all_to_all x1, blocking collectives, sum_at_owner(): tiles = lax.all_to_all(split_up(x, dim, count), axis, 0, 0, tiled=True)  18.8 us
    all_to_all x1, starting transfers between devices, sum_at_owner(): tiles = lax.all_to_all(split_up(x, dim, count), axis, 0, 0, tiled=True)  11.6 us
    select_n x16, other arithmetic, advance(): id_block[:, None] // 128 == high_levels[None, :]  11.3 us
    all_to_all x1, waiting for transfers between devices, from_everyone(): lax.all_to_all(jnp.broadcast_to(x[None], (count, *x.shape)), axis, 0, 0,...  9.96 us
    all_to_all x1, waiting for transfers between devices, sum_at_owner(): tiles = lax.all_to_all(split_up(x, dim, count), axis, 0, 0, tiled=True)  9.32 us
  transfers between devices with their start and end apart: 2, of which 2 were waited for; matrix products, arithmetic and copies ran while one was open for 0% of the time, Pallas kernels for 0%

commit v1 on v0

v1 whole, which is shorter than its diff:
```python
import functools

import jax
import jax.numpy as jnp
from jax import lax
from jax.experimental import pallas as pl
from jax.experimental.pallas import tpu as pltpu
from jax.sharding import PartitionSpec as P

BINS = 64
LEAVES = 32
F8 = jnp.float8_e4m3fn
BF = jnp.bfloat16
F32 = jnp.float32
I32 = jnp.int32
MESH = pl.DeviceIdType.MESH
NT = (((1,), (1,)), ((), ()))
NY, NZ, NF = 4, 8, 8
LO, HI = 64, 256
CHUNKS = 4
PARTS = (20, 46, 64)


def iota0(dtype, rows, lanes):
    return lax.broadcasted_iota(I32, (rows, lanes), 0).astype(dtype)


def split(value, count):
    terms = []
    for _ in range(count):
        term = value.astype(BF).astype(F32)
        terms.append(term)
        value = value - term
    return terms


def kernel(
    g_ref, h_ref, group_ref, leaf_ref, size_ref, ratio_ref, bins_hbm,
    hist_ref, mean_ref,
    bins_ref, high_ref, hot_ref, left_ref,
    pay_ref, pay_in, mid_ref, mid_in, table_ref,
    out_y, in_y, out_z, in_z,
    bins_sem, ps, pr, ms, mr, ts, tr, ys, yr, zs, zr,
):
    rows, feat = lax.axis_index("rows"), lax.axis_index("feat")
    z, y = rows // NY, lax.rem(rows, NY)

    def y_peer(k):
        return (z * NY + lax.rem(y + k, NY), feat)

    def z_peer(k):
        return (lax.rem(z + k, NZ) * NY + y, feat)

    def f_peer(k):
        return (rows, lax.rem(feat + k, NF))

    def send(src, dst, send_sem, recv_sem, peer):
        return pltpu.make_async_remote_copy(
            src_ref=src, dst_ref=dst, send_sem=send_sem, recv_sem=recv_sem,
            device_id=peer, device_id_type=MESH,
        )

    fetch = pltpu.make_async_copy(bins_hbm, bins_ref, bins_sem)
    fetch.start()
    barrier = pltpu.get_barrier_semaphore()
    for peer in (
        [y_peer(k) for k in range(1, NY)]
        + [z_peer(k) for k in range(1, NZ)]
        + [f_peer(k) for k in range(1, NF)]
    ):
        pl.semaphore_signal(barrier, inc=1, device_id=peer, device_id_type=MESH)

    def hot_high(ids):
        wide = jnp.broadcast_to(ids // LO, (HI, 128)).astype(jnp.int16)
        return jnp.where(wide == iota0(jnp.int16, HI, 128), BF(1), BF(0))

    def low_rows(ids, values):
        own = jnp.broadcast_to(lax.rem(ids, LO) - 8 * feat, (8, 128)) == iota0(I32, 8, 128)
        return [jnp.where(own, jnp.broadcast_to(v, (8, 128)), 0.0) for v in values]

    def sum_step(t, total):
        left, right = [], []
        for u in range(4):
            row = pl.ds(4 * t + u, 1)
            ids = group_ref[row, :]
            hot = hot_high(ids)
            high_ref[:, pl.ds(pl.multiple_of(512 * t + 128 * u, 128), 128)] = hot
            right.append(hot)
            left.append(jnp.concatenate(low_rows(ids, split(g_ref[row, :], 3)), 0).astype(BF))
        return total + lax.dot_general(
            jnp.concatenate(left, 1), jnp.concatenate(right, 1), NT, preferred_element_type=F32
        )

    total = lax.fori_loop(0, 32, sum_step, jnp.zeros((24, HI), F32))
    pay_ref[0:8, :] = total[0:8] + total[8:16] + total[16:24]
    left, right = [], []
    for u in range(4):
        ids = 512 * rows + 128 * u + lax.broadcasted_iota(I32, (1, 128), 1)
        right.append(hot_high(ids))
        left.append(low_rows(ids, [size_ref[u : u + 1, :]])[0].astype(BF))
    pay_ref[8:16, :] = lax.dot_general(
        jnp.concatenate(left, 1), jnp.concatenate(right, 1), NT, preferred_element_type=F32
    )

    pl.semaphore_wait(barrier, NY + NZ + NF - 3)

    def hot_step(t, _):
        lanes = pl.ds(pl.multiple_of(256 * t, 256), 256)
        for f in range(32):
            wide = jnp.broadcast_to(bins_ref[f : f + 1, lanes], (BINS, 256)).astype(jnp.int8)
            hot_ref[BINS * f : BINS * (f + 1), lanes] = jnp.where(
                wide == iota0(jnp.int8, BINS, 256), F8(1), F8(0)
            )
        return 0

    def build(first, last):
        lax.fori_loop(first, last, hot_step, 0)

    copies = [
        send(pay_ref, pay_in.at[k - 1], ps.at[k - 1], pr.at[k - 1], y_peer(k))
        for k in range(1, NY)
    ]
    for copy in copies:
        copy.start()
    fetch.wait()
    build(0, PARTS[0])
    for copy in copies:
        copy.wait()
    mid_ref[...] = pay_ref[...] + pay_in[0] + pay_in[1] + pay_in[2]

    copies = [
        send(mid_ref, mid_in.at[k - 1], ms.at[k - 1], mr.at[k - 1], z_peer(k))
        for k in range(1, NZ)
    ]
    for copy in copies:
        copy.start()
    build(PARTS[0], PARTS[1])
    for copy in copies:
        copy.wait()
    total = mid_ref[...]
    for k in range(NZ - 1):
        total = total + mid_in[k]
    mine = pl.ds(pl.multiple_of(8 * feat, 8), 8)
    table_ref[mine, :] = -total[0:8] / (total[8:16] + ratio_ref[0])

    copies = [
        send(table_ref.at[mine], table_ref.at[mine], ts.at[k - 1], tr.at[k - 1], f_peer(k))
        for k in range(1, NF)
    ]
    for copy in copies:
        copy.start()
    build(PARTS[1], PARTS[2])
    for copy in copies:
        copy.wait()

    table = table_ref[...]
    terms = split(table, 3)
    wanted = lax.broadcasted_iota(I32, (8, HI), 1) - 8 * rows
    line = lax.broadcasted_iota(I32, (8, HI), 0)
    halves = []
    for half in range(2):
        pick = jnp.where(wanted == 2 * line + half, 1.0, 0.0).astype(BF)
        halves.append(
            sum(
                lax.dot_general(pick, term.astype(BF), NT, preferred_element_type=F32)
                for term in terms
            )
        )
    mean_ref[...] = jnp.concatenate(halves, 1)[0:4]
    bound = jnp.max(jnp.max(jnp.abs(table), axis=0, keepdims=True), axis=1, keepdims=True) + 6.0
    left_over = bound * 2.0**60
    scale = jnp.full_like(bound, 2.0**60)
    for step in (64, 32, 16, 8, 4, 2, 1):
        large = left_over >= 2.0**step
        left_over = jnp.where(large, left_over * 2.0**-step, left_over)
        scale = jnp.where(large, scale * 2.0**-step, scale)
    back = jnp.full_like(scale, 2.0**-7) / scale
    scale = scale * 2.0**7
    table2 = jnp.concatenate(terms[0:2], 0).astype(BF)

    def left_step(t, _):
        lanes = pl.ds(pl.multiple_of(256 * t, 256), 256)
        found = jnp.dot(table2, high_ref[:, lanes], preferred_element_type=F32)
        found = found[0:LO] + found[LO : 2 * LO]
        for u in range(2):
            row = pl.ds(2 * t + u, 1)
            part = found[:, 128 * u : 128 * (u + 1)]
            low = jnp.broadcast_to(lax.rem(group_ref[row, :], LO), (LO, 128))
            part = jnp.where(low == iota0(I32, LO, 128), part, 0.0)
            mean = jnp.sum(part, axis=0, keepdims=True)
            hess = h_ref[row, :]
            adjusted = (g_ref[row, :] + hess * mean).astype(BF).astype(F32) * scale
            hess = hess * 128.0
            leaf = leaf_ref[row, :]
            place = lax.rem(leaf, NY) * NZ + leaf // NY
            wide = jnp.broadcast_to(place, (LEAVES, 128)).astype(jnp.int8)
            member = wide == iota0(jnp.int8, LEAVES, 128)
            at = pl.ds(pl.multiple_of(256 * t + 128 * u, 128), 128)
            for c, value in enumerate((adjusted, hess)):
                first = value.astype(F8)
                second = ((value - first.astype(F32)) * 16.0).astype(F8).astype(F32)
                for p, term in enumerate((first.astype(F32), second)):
                    term = jnp.broadcast_to(term, (LEAVES, 128)).astype(F8)
                    begin = LEAVES * (2 * c + p)
                    left_ref[begin : begin + LEAVES, at] = jnp.where(member, term, F8(0))
        return 0

    lax.fori_loop(0, 64, left_step, 0)

    low_half = lax.broadcasted_iota(I32, (8, 128), 1) < BINS

    def histogram(c):
        def step(n, _):
            block = 2 * c + n
            hot = hot_ref[pl.ds(pl.multiple_of(256 * block, 256), 256), :]
            both = lax.dot_general(left_ref[...], hot, NT, preferred_element_type=F32)
            grad = (both[0:32] + both[32:64] * 0.0625) * back
            hess = (both[64:96] + both[96:128] * 0.0625) * (1.0 / 128.0)
            for to in range(NY):
                for pair in range(2):
                    a = grad[8 * to : 8 * to + 8, 128 * pair : 128 * pair + 128]
                    b = hess[8 * to : 8 * to + 8, 128 * pair : 128 * pair + 128]
                    out_y[c, to, 4 * n + 2 * pair] = jnp.where(low_half, a, pltpu.roll(b, 64, 1))
                    out_y[c, to, 4 * n + 2 * pair + 1] = jnp.where(low_half, pltpu.roll(a, 64, 1), b)
            return 0

        lax.fori_loop(0, 2, step, 0)

    def y_copies(c):
        return [
            send(
                out_y.at[c, lax.rem(y + k, NY)], in_y.at[c, k - 1],
                ys.at[c, k - 1], yr.at[c, k - 1], y_peer(k),
            )
            for k in range(1, NY)
        ]

    def z_copies(c):
        return [
            send(
                out_z.at[c, pl.ds(pl.multiple_of(8 * lax.rem(z + k, NZ), 8), 8)],
                in_z.at[c, k - 1], zs.at[c, k - 1], zr.at[c, k - 1], z_peer(k),
            )
            for k in range(1, NZ)
        ]

    def second_stage(c):
        for copy in y_copies(c):
            copy.wait()
        for f in range(8):
            part = out_y[c, y, f] + in_y[c, 0, f] + in_y[c, 1, f] + in_y[c, 2, f]
            out_z[c, pl.ds(f, 8, stride=8), :] = part
        for copy in z_copies(c):
            copy.start()

    def finish(c):
        for copy in z_copies(c):
            copy.wait()
        part = out_z[c, pl.ds(pl.multiple_of(8 * z, 8), 8), :]
        for k in range(NZ - 1):
            part = part + in_z[c, k]
        hist_ref[8 * c : 8 * c + 8, :] = part

    for c in range(CHUNKS):
        histogram(c)
        for copy in y_copies(c):
            copy.start()
        if c >= 2:
            second_stage(c - 2)
    second_stage(CHUNKS - 2)
    second_stage(CHUNKS - 1)
    for c in range(CHUNKS):
        finish(c)


def shards(gradient, hessian, groups, leaf_ids, bins, group_sizes, variance_ratio):
    count = gradient.shape[0]
    vmem, sem = pltpu.VMEM, pltpu.SemaphoreType.DMA
    whole = pl.BlockSpec(memory_space=pltpu.VMEM)
    hist, means = pl.pallas_call(
        kernel,
        out_shape=(jax.ShapeDtypeStruct((32, 128), F32), jax.ShapeDtypeStruct((4, 128), F32)),
        in_specs=[whole] * 5
        + [pl.BlockSpec(memory_space=pltpu.SMEM), pl.BlockSpec(memory_space=pl.ANY)],
        out_specs=(whole, whole),
        scratch_shapes=[
            vmem((32, count), I32),
            vmem((HI, count), BF),
            vmem((32 * BINS, count), F8),
            vmem((4 * LEAVES, count), F8),
            vmem((16, HI), F32),
            vmem((NY - 1, 16, HI), F32),
            vmem((16, HI), F32),
            vmem((NZ - 1, 16, HI), F32),
            vmem((LO, HI), F32),
            vmem((CHUNKS, NY, 8, 8, 128), F32),
            vmem((CHUNKS, NY - 1, 8, 8, 128), F32),
            vmem((CHUNKS, 64, 128), F32),
            vmem((CHUNKS, NZ - 1, 8, 128), F32),
            sem,
            sem((NY - 1,)), sem((NY - 1,)),
            sem((NZ - 1,)), sem((NZ - 1,)),
            sem((NF - 1,)), sem((NF - 1,)),
            sem((CHUNKS, NY - 1)), sem((CHUNKS, NY - 1)),
            sem((CHUNKS, NZ - 1)), sem((CHUNKS, NZ - 1)),
        ],
        compiler_params=pltpu.CompilerParams(
            collective_id=0, has_side_effects=True, vmem_limit_bytes=62 * 1024 * 1024
        ),
    )(
        gradient.reshape(128, 128),
        hessian.astype(F32).reshape(128, 128),
        groups.reshape(128, 128),
        leaf_ids.reshape(128, 128),
        group_sizes.astype(F32).reshape(4, 128),
        variance_ratio,
        bins,
    )
    return hist.reshape(1, 32, 128), means.reshape(512)


def solution(mesh):
    in_specs = (P("rows"), P("rows"), P("rows"), P("rows"), P("feat", "rows"), P("rows"), P())
    out_specs = (P("rows", "feat", None), P("rows"))
    return jax.shard_map(shards, mesh=mesh, in_specs=in_specs, out_specs=out_specs, check_vma=False)
```

time: 183 us -> 66.6 us (0.36)
  the two profiles are of different devices: /device:TPU:4 before, /device:TPU:1 now
where the time goes in v1:
time: 66.6 us; the launch traced here: 66.3 us
  Pallas kernels  59.7 us (90%)
  other arithmetic  2.64 us (4%)
  local copies, waits for them, and re-layouts  2.59 us (4%)
  between operations  1.29 us (2%)
    pallas_call x1, Pallas kernels, shards(): pl.pallas_call(kernel, out_shape=(jax.ShapeDtypeStruct((32, 128), F32), j...  59.7 us
    unnamed x2, local copies, waits for them, and re-layouts  2.59 us
    reshape x1, other arithmetic, shards(): hessian.astype(F32).reshape(128, 128)  1.38 us

profile of v1, /device:TPU:1, one launch (start us, length us, event | category | flops | bytes accessed | tf_op | source)
XLA Modules:
  0.0 66.3 jit_solution(3915493308462737547)
XLA Ops:
  1.3 1.3 %convert_bitcast_fusion.size_ref = f32[4,128]{1,0:T(4,128)} fusion(s32[512]{0:T(512)} %param.12), kind=kLoop, calls=%fused_computation.1 | loop fusion | flops 512 | bytes 4096 | tf_op jit(solution)/shard_map/reshape | solution.py:315
  2.5 1.4 %bitcast_convert_fusion.h_ref = f32[128,128]{1,0:T(8,128)} fusion(bf16[16384]{0:T(1024)(128)(2,1)} %param.8), kind=kLoop, calls=%fused_computation | loop fusion | flops 16384 | bytes 98304 | tf_op jit(solution)/shard_map/reshape | solution.py:312
  3.9 59.7 %shard_map.86 = (f32[32,128]{1,0:T(8,128)}, f32[4,128]{1,0:T(4,128)}) custom-call(f32[128,128]{1,0:T(8,128)} %bitcast.10, f32[128,128]{1,0:T(8,128)} %bitcast_convert_fusion.h_ref, s32[128,128]{1,0:T(8,128)} %bitcast.11, s32[128,128]{1,0:T(8,128)} %bitcast.12, f32[4,128]{1,0:T(4,128)} %convert_bitcast_fusion.size_ref, f32[1]{0:T(128)S(6)} %copy.11.ratio_ref, ...), custom_call_target="tpu_custom_call" | custom-call | tf_op jit(solution)/shard_map/pallas_call | solution.py:280
  63.7 1.3 %copy.12 = f32[1,32,128]{2,1,0:T(8,128)} copy(f32[1,32,128]{2,1,0:T(8,128)} %bitcast.13) | data formatting | bytes 32768
  65.0 1.3 %copy.13 = f32[512]{0:T(512)} copy(f32[512]{0:T(512)} %bitcast.14) | data formatting | bytes 4096

commit v2 on v1

v2 whole, which is shorter than its diff:
```python
import functools

import jax
import jax.numpy as jnp
from jax import lax
from jax.experimental import pallas as pl
from jax.experimental.pallas import tpu as pltpu
from jax.sharding import PartitionSpec as P

BINS = 64
LEAVES = 32
F8 = jnp.float8_e4m3fn
BF = jnp.bfloat16
F32 = jnp.float32
I32 = jnp.int32
MESH = pl.DeviceIdType.MESH
NT = (((1,), (1,)), ((), ()))
NY, NZ, NF = 4, 8, 8
BLOCKS = 4
CHUNKS = 4
PARTS = (20, 46, 64)


def iota0(dtype, rows, lanes):
    return lax.broadcasted_iota(I32, (rows, lanes), 0).astype(dtype)


def split(value, count):
    terms = []
    for _ in range(count):
        term = value.astype(BF).astype(F32)
        terms.append(term)
        value = value - term
    return terms


def kernel(
    g_ref, h_ref, group_ref, leaf_ref, size_ref, ratio_ref, bins_hbm,
    hist_ref, mean_ref,
    bins_ref, hot_ref, left_ref, low_hot_ref,
    ids_ref, term_ref, row_mean_ref,
    pay_ref, pay_in, mid_ref, mid_in, own_size_ref, size_y_ref, size_z_ref, size_in_ref, table_ref,
    out_y, in_y, out_z, in_z,
    bins_sem, ps, pr, ms, mr, ts, tr, ss, sr, us, ur, ys, yr, zs, zr,
):
    rows, feat = lax.axis_index("rows"), lax.axis_index("feat")
    z, y = rows // NY, lax.rem(rows, NY)

    def y_peer(k):
        return (z * NY + lax.rem(y + k, NY), feat)

    def z_peer(k):
        return (lax.rem(z + k, NZ) * NY + y, feat)

    def f_peer(k):
        return (rows, lax.rem(feat + k, NF))

    def send(src, dst, send_sem, recv_sem, peer):
        return pltpu.make_async_remote_copy(
            src_ref=src, dst_ref=dst, send_sem=send_sem, recv_sem=recv_sem,
            device_id=peer, device_id_type=MESH,
        )

    barrier = pltpu.get_barrier_semaphore()
    for peer in (
        [y_peer(k) for k in range(1, NY)]
        + [z_peer(k) for k in range(1, NZ)]
        + [f_peer(k) for k in range(1, NF)]
    ):
        pl.semaphore_signal(barrier, inc=1, device_id=peer, device_id_type=MESH)
    fetch = pltpu.make_async_copy(bins_hbm, bins_ref, bins_sem)
    fetch.start()

    ids = group_ref[...]
    high, low = lax.shift_right_logical(ids, 7), ids & 127
    ids_ref[0] = high - 16 * feat
    ids_ref[1] = low
    ids_ref[2] = low + 2 * (high & 64)
    ids_ref[3] = high & 63
    leaf = leaf_ref[...]
    ids_ref[4] = (leaf & (NY - 1)) * NZ + lax.shift_right_logical(leaf, 2)
    for n, term in enumerate(split(g_ref[...], 3)):
        term_ref[n] = term
    left, right = [], []
    for t in range(128):
        row = slice(t, t + 1)
        wide = jnp.broadcast_to(ids_ref[1, row, :], (128, 128)).astype(jnp.int16)
        right.append(jnp.where(wide == iota0(jnp.int16, 128, 128), BF(1), BF(0)))
        wide = jnp.broadcast_to(ids_ref[0, row, :], (16, 128)).astype(jnp.int16)
        own = wide == iota0(jnp.int16, 16, 128)
        values = [
            jnp.where(own, jnp.broadcast_to(term_ref[n, row, :], (16, 128)).astype(BF), BF(0))
            for n in range(3)
        ]
        left.append(jnp.concatenate(values, 0))
    total = lax.dot_general(
        jnp.concatenate(left, 1), jnp.concatenate(right, 1), NT, preferred_element_type=F32
    )
    pay_ref[...] = total[0:16] + total[16:32] + total[32:48]
    own_size_ref[...] = size_ref[...].astype(F32)

    with jax.named_scope("bar"):
        pl.semaphore_wait(barrier, NY + NZ + NF - 3)

    def hot_step(t, _):
        lanes = pl.ds(pl.multiple_of(256 * t, 256), 256)
        for f in range(32):
            wide = jnp.broadcast_to(bins_ref[f : f + 1, lanes], (BINS, 256)).astype(jnp.int8)
            hot_ref[BINS * f : BINS * (f + 1), lanes] = jnp.where(
                wide == iota0(jnp.int8, BINS, 256), F8(1), F8(0)
            )
        return 0

    def build(first, last):
        with jax.named_scope("build"):
            lax.fori_loop(first, last, hot_step, 0)

    def left_rows(parts):
        def step(t, _):
            for u in range(16):
                row = pl.ds(16 * t + u, 1)
                wide = jnp.broadcast_to(ids_ref[4, row, :], (LEAVES, 128)).astype(jnp.int8)
                member = wide == iota0(jnp.int8, LEAVES, 128)
                at = pl.ds(pl.multiple_of(2048 * t + 128 * u, 128), 128)
                for c in parts:
                    term = jnp.broadcast_to(term_ref[c, row, :], (LEAVES, 128)).astype(F8)
                    left_ref[LEAVES * c : LEAVES * (c + 1), at] = jnp.where(member, term, F8(0))
            return 0

        with jax.named_scope("left"):
            lax.fori_loop(0, 8, step, 0)

    def left_terms(c, value):
        first = value.astype(F8).astype(F32)
        term_ref[c] = first
        term_ref[c + 1] = ((value - first) * 16.0).astype(F8).astype(F32)

    copies = [
        send(pay_ref, pay_in.at[k - 1], ps.at[k - 1], pr.at[k - 1], y_peer(k))
        for k in range(1, NY)
    ]
    for copy in copies:
        copy.start()
    sizes = [
        send(own_size_ref, size_y_ref.at[y], ss.at[k - 1], sr.at[k - 1], y_peer(k))
        for k in range(1, NY)
    ]
    for copy in sizes:
        copy.start()
    with jax.named_scope("fetch"):
        fetch.wait()
    build(0, PARTS[0])
    with jax.named_scope("cwait"):
        for copy in copies:
            copy.wait()
    mid_ref[...] = pay_ref[...] + pay_in[0] + pay_in[1] + pay_in[2]

    copies = [
        send(mid_ref, mid_in.at[k - 1], ms.at[k - 1], mr.at[k - 1], z_peer(k))
        for k in range(1, NZ)
    ]
    for copy in copies:
        copy.start()
    for copy in sizes:
        copy.wait()
    size_y_ref[y] = own_size_ref[...]
    for k in range(NY):
        size_z_ref[4 * k : 4 * k + 4, :] = size_y_ref[k]

    def size_copies():
        return [
            send(size_z_ref, size_in_ref, us.at[k - 1], ur, z_peer(k)) for k in range(1, NZ)
        ]

    @pl.when(z == feat)
    def _():
        for copy in size_copies():
            copy.start()

    build(PARTS[0], PARTS[1])

    def low_hot_step(t, _):
        for u in range(4):
            wide = jnp.broadcast_to(ids_ref[2, pl.ds(4 * t + u, 1), :], (256, 128))
            at = pl.ds(pl.multiple_of(512 * t + 128 * u, 128), 128)
            low_hot_ref[:, at] = jnp.where(
                wide.astype(jnp.int16) == iota0(jnp.int16, 256, 128), BF(1), BF(0)
            )
        return 0

    with jax.named_scope("lowhot"):
        lax.fori_loop(0, 32, low_hot_step, 0)
    hess = h_ref[...].astype(F32)
    left_terms(2, hess * 128.0)
    left_rows((2, 3))
    with jax.named_scope("cwait"):
        for copy in copies:
            copy.wait()
    @pl.when(z == feat)
    def _():
        for copy in size_copies():
            copy.wait_send()
        size_in_ref[...] = size_z_ref[...]

    @pl.when(z != feat)
    def _():
        size_copies()[0].wait_recv()
    total = mid_ref[...]
    for k in range(NZ - 1):
        total = total + mid_in[k]
    mine = pl.ds(pl.multiple_of(16 * feat, 16), 16)
    table_ref[mine, :] = -total / (size_in_ref[...] + ratio_ref[0])

    copies = [
        send(table_ref.at[mine], table_ref.at[mine], ts.at[k - 1], tr.at[k - 1], f_peer(k))
        for k in range(1, NF)
    ]
    for copy in copies:
        copy.start()
    build(PARTS[1], PARTS[2])
    with jax.named_scope("cwait"):
        for copy in copies:
            copy.wait()

    table = table_ref[...]
    mean_ref[...] = table_ref[pl.ds(pl.multiple_of(4 * rows, 4), 4), :]
    wide = jnp.concatenate([table[0:64], table[64:128]], 1)
    wide = jnp.concatenate(split(wide, 2), 0).astype(BF)
    with jax.named_scope("look"):
        for block in range(BLOCKS):
            span = 16384 // BLOCKS
            found = jnp.dot(
                wide, low_hot_ref[:, span * block : span * (block + 1)], preferred_element_type=F32
            )
            for u in range(span // 128):
                row = slice(block * (span // 128) + u, block * (span // 128) + u + 1)
                at = slice(128 * u, 128 * u + 128)
                part = found[0:64, at] + found[64:128, at]
                own = jnp.broadcast_to(ids_ref[3, row, :], (64, 128)) == iota0(I32, 64, 128)
                row_mean_ref[row, :] = jnp.sum(jnp.where(own, part, 0.0), axis=0, keepdims=True)
    bound = jnp.max(jnp.max(jnp.abs(table), axis=0, keepdims=True), axis=1, keepdims=True) + 6.0
    left_over = bound * 2.0**60
    scale = jnp.full_like(bound, 2.0**60)
    for step in (64, 32, 16, 8, 4, 2, 1):
        large = left_over >= 2.0**step
        left_over = jnp.where(large, left_over * 2.0**-step, left_over)
        scale = jnp.where(large, scale * 2.0**-step, scale)
    back = jnp.full_like(scale, 2.0**-7) / scale
    scale = scale * 2.0**7
    adjusted = (g_ref[...] + hess * row_mean_ref[...]).astype(BF).astype(F32)
    left_terms(0, adjusted * scale)
    left_rows((0, 1))

    low_half = lax.broadcasted_iota(I32, (8, 128), 1) < BINS

    def histogram(c):
        def step(n, _):
            block = 2 * c + n
            hot = hot_ref[pl.ds(pl.multiple_of(256 * block, 256), 256), :]
            both = lax.dot_general(left_ref[...], hot, NT, preferred_element_type=F32)
            grad = (both[0:32] + both[32:64] * 0.0625) * back
            hess = (both[64:96] + both[96:128] * 0.0625) * (1.0 / 128.0)
            for to in range(NY):
                for pair in range(2):
                    a = grad[8 * to : 8 * to + 8, 128 * pair : 128 * pair + 128]
                    b = hess[8 * to : 8 * to + 8, 128 * pair : 128 * pair + 128]
                    out_y[c, to, 4 * n + 2 * pair] = jnp.where(low_half, a, pltpu.roll(b, 64, 1))
                    out_y[c, to, 4 * n + 2 * pair + 1] = jnp.where(low_half, pltpu.roll(a, 64, 1), b)
            return 0

        with jax.named_scope("mm"):
            lax.fori_loop(0, 2, step, 0)

    def y_copies(c):
        return [
            send(
                out_y.at[c, lax.rem(y + k, NY)], in_y.at[c, k - 1],
                ys.at[c, k - 1], yr.at[c, k - 1], y_peer(k),
            )
            for k in range(1, NY)
        ]

    def z_copies(c):
        return [
            send(
                out_z.at[c, pl.ds(pl.multiple_of(8 * lax.rem(z + k, NZ), 8), 8)],
                in_z.at[c, k - 1], zs.at[c, k - 1], zr.at[c, k - 1], z_peer(k),
            )
            for k in range(1, NZ)
        ]

    def second_stage(c):
        with jax.named_scope("ywait"):
            for copy in y_copies(c):
                copy.wait()
        for f in range(8):
            part = out_y[c, y, f] + in_y[c, 0, f] + in_y[c, 1, f] + in_y[c, 2, f]
            out_z[c, pl.ds(f, 8, stride=8), :] = part
        for copy in z_copies(c):
            copy.start()

    def finish(c):
        with jax.named_scope("zwait"):
            for copy in z_copies(c):
                copy.wait()
        part = out_z[c, pl.ds(pl.multiple_of(8 * z, 8), 8), :]
        for k in range(NZ - 1):
            part = part + in_z[c, k]
        hist_ref[8 * c : 8 * c + 8, :] = part

    for c in range(CHUNKS):
        histogram(c)
        for copy in y_copies(c):
            copy.start()
        if c >= 2:
            second_stage(c - 2)
    second_stage(CHUNKS - 2)
    second_stage(CHUNKS - 1)
    for c in range(CHUNKS):
        finish(c)


def shards(gradient, hessian, groups, leaf_ids, bins, group_sizes, variance_ratio):
    count = gradient.shape[0]
    vmem, sem = pltpu.VMEM, pltpu.SemaphoreType.DMA
    whole = pl.BlockSpec(memory_space=pltpu.VMEM)
    hist, means = pl.pallas_call(
        kernel,
        out_shape=(jax.ShapeDtypeStruct((32, 128), F32), jax.ShapeDtypeStruct((4, 128), F32)),
        in_specs=[whole] * 5
        + [pl.BlockSpec(memory_space=pltpu.SMEM), pl.BlockSpec(memory_space=pl.ANY)],
        out_specs=(whole, whole),
        scratch_shapes=[
            vmem((32, count), I32),
            vmem((32 * BINS, count), F8),
            vmem((4 * LEAVES, count), F8),
            vmem((256, count), BF),
            vmem((5, 128, 128), I32),
            vmem((4, 128, 128), F32),
            vmem((128, 128), F32),
            vmem((16, 128), F32),
            vmem((NY - 1, 16, 128), F32),
            vmem((16, 128), F32),
            vmem((NZ - 1, 16, 128), F32),
            vmem((4, 128), F32),
            vmem((NY, 4, 128), F32),
            vmem((16, 128), F32),
            vmem((16, 128), F32),
            vmem((128, 128), F32),
            vmem((CHUNKS, NY, 8, 8, 128), F32),
            vmem((CHUNKS, NY - 1, 8, 8, 128), F32),
            vmem((CHUNKS, 64, 128), F32),
            vmem((CHUNKS, NZ - 1, 8, 128), F32),
            sem,
            sem((NY - 1,)), sem((NY - 1,)),
            sem((NZ - 1,)), sem((NZ - 1,)),
            sem((NF - 1,)), sem((NF - 1,)),
            sem((NY - 1,)), sem((NY - 1,)),
            sem((NZ - 1,)), sem,
            sem((CHUNKS, NY - 1)), sem((CHUNKS, NY - 1)),
            sem((CHUNKS, NZ - 1)), sem((CHUNKS, NZ - 1)),
        ],
        compiler_params=pltpu.CompilerParams(
            collective_id=0, has_side_effects=True, vmem_limit_bytes=56 * 1024 * 1024
        ),
    )(
        gradient.reshape(128, 128),
        hessian.reshape(128, 128),
        groups.reshape(128, 128),
        leaf_ids.reshape(128, 128),
        group_sizes.reshape(4, 128),
        variance_ratio,
        bins,
    )
    return hist.reshape(1, 32, 128), means.reshape(512)


def solution(mesh):
    in_specs = (P("rows"), P("rows"), P("rows"), P("rows"), P("feat", "rows"), P("rows"), P())
    out_specs = (P("rows", "feat", None), P("rows"))
    return jax.shard_map(shards, mesh=mesh, in_specs=in_specs, out_specs=out_specs, check_vma=False)
```

time: 66.6 us -> 49.2 us (0.74)
  Pallas kernels: 59.7 us -> 45.1 us
  other arithmetic: 2.64 us -> 0 us
    pallas_call x1, Pallas kernels: 59.7 us -> 45.1 us  [shards(): pl.pallas_call(kernel, out_shape=(jax.ShapeDtypeStruct((32, 128), F32), j...]
    reshape x2 -> x0, other arithmetic: 2.64 us -> none  [the longest x1 1.38 us: shards(): hessian.astype(F32).reshape(128, 128)]
where the time goes in v2:
time: 49.2 us; the launch traced here: 49 us
  Pallas kernels  45.1 us (92%)
  local copies, waits for them, and re-layouts  2.55 us (5%)
  between operations  1.29 us (3%)
    pallas_call x1, Pallas kernels, shards(): pl.pallas_call(kernel, out_shape=(jax.ShapeDtypeStruct((32, 128), F32), j...  45.1 us
    unnamed x2, local copies, waits for them, and re-layouts  2.55 us

profile of v2, /device:TPU:1, one launch (start us, length us, event | category | flops | bytes accessed | tf_op | source)
XLA Modules:
  0.0 49.0 jit_solution(5172692527308843203)
XLA Ops:
  1.3 45.1 %shard_map.86 = (f32[32,128]{1,0:T(8,128)}, f32[4,128]{1,0:T(4,128)}) custom-call(f32[128,128]{1,0:T(8,128)} %bitcast.7, bf16[128,128]{1,0:T(8,128)(2,1)} %bitcast.10, s32[128,128]{1,0:T(8,128)} %bitcast.8, s32[128,128]{1,0:T(8,128)} %bitcast.9, s32[4,128]{1,0:T(4,128)} %bitcast.13, f32[1]{0:T(128)S(6)} %copy.11.ratio_ref, s32[32,16384]{1,0:T(8,128)} %bins_hbm.1), custom_call_target="tpu_custom_call" | custom-call | tf_op jit(solution)/shard_map/pallas_call | solution.py:327
  46.4 1.3 %copy.12 = f32[1,32,128]{2,1,0:T(8,128)} copy(f32[1,32,128]{2,1,0:T(8,128)} %bitcast.11) | data formatting | bytes 32768
  47.8 1.2 %copy.13 = f32[512]{0:T(512)} copy(f32[512]{0:T(512)} %bitcast.12) | data formatting | bytes 4096

commit v3 on v2

v3 whole, which is shorter than its diff:
```python
import functools

import jax
import jax.numpy as jnp
from jax import lax
from jax.experimental import pallas as pl
from jax.experimental.pallas import tpu as pltpu
from jax.sharding import PartitionSpec as P

BINS = 64
LEAVES = 32
F8 = jnp.float8_e4m3fn
BF = jnp.bfloat16
F32 = jnp.float32
I32 = jnp.int32
MESH = pl.DeviceIdType.MESH
NT = (((1,), (1,)), ((), ()))
NY, NZ, NF = 4, 8, 8
BLOCKS = 2
SUM_ROWS = 64
CHUNKS = 4
PARTS = (4, 46, 64)


def iota0(dtype, rows, lanes):
    return lax.broadcasted_iota(I32, (rows, lanes), 0).astype(dtype)


def split(value, count):
    terms = []
    for _ in range(count):
        term = value.astype(BF).astype(F32)
        terms.append(term)
        value = value - term
    return terms


def kernel(
    g_ref, h_ref, group_ref, leaf_ref, size_ref, ratio_ref, bins_hbm,
    parts_ref, mean_ref,
    bins_ref, hot_ref, left_ref, low_hot_ref,
    ids_ref, term_ref, row_mean_ref,
    pay_ref, pay_in, mid_ref, mid_in, own_size_ref, size_in_y, size_z_ref, size_in_ref, table_ref,
    out_y, in_y, out_z,
    bins_sem, mean_sem, own_sem, send_sem, recv_sem, y_send, y_recv, z_send, z_recv,
):
    rows, feat = lax.axis_index("rows"), lax.axis_index("feat")
    z, y = rows // NY, lax.rem(rows, NY)

    def y_peer(k):
        return (z * NY + lax.rem(y + k, NY), feat)

    def z_peer(k):
        return (lax.rem(z + k, NZ) * NY + y, feat)

    def f_peer(k):
        return (rows, lax.rem(feat + k, NF))

    def send(src, dst, sems, peer):
        return pltpu.make_async_remote_copy(
            src_ref=src, dst_ref=dst, send_sem=sems[0], recv_sem=sems[1],
            device_id=peer, device_id_type=MESH,
        )

    def wait(ref, sem):
        pltpu.make_async_copy(ref, ref, sem).wait()

    def wait_both(ref, sems):
        for sem in sems:
            wait(ref, sem)

    pay_sems, size_sems, mid_sems, far_sems, table_sems = [
        (send_sem.at[n], recv_sem.at[n]) for n in range(5)
    ]

    barrier = pltpu.get_barrier_semaphore()
    for peer in (
        [y_peer(k) for k in range(1, NY)]
        + [z_peer(k) for k in range(1, NZ)]
        + [f_peer(k) for k in range(1, NF)]
    ):
        pl.semaphore_signal(barrier, inc=1, device_id=peer, device_id_type=MESH)
    fetch = pltpu.make_async_copy(bins_hbm, bins_ref, bins_sem)
    fetch.start()

    ids = group_ref[...]
    high, low = lax.shift_right_logical(ids, 7), ids & 127
    ids_ref[0] = high - 16 * feat
    ids_ref[1] = low
    ids_ref[2] = low + 2 * (high & 64)
    ids_ref[3] = high & 63
    leaf = leaf_ref[...]
    ids_ref[4] = (leaf & (NY - 1)) * NZ + lax.shift_right_logical(leaf, 2)
    for n, term in enumerate(split(g_ref[...], 3)):
        term_ref[n] = term

    def sum_step(n, total):
        left, right = [], []
        for t in range(SUM_ROWS):
            row = pl.ds(SUM_ROWS * n + t, 1)
            wide = jnp.broadcast_to(ids_ref[1, row, :], (128, 128)).astype(jnp.int16)
            right.append(jnp.where(wide == iota0(jnp.int16, 128, 128), BF(1), BF(0)))
            wide = jnp.broadcast_to(ids_ref[0, row, :], (16, 128)).astype(jnp.int16)
            own = wide == iota0(jnp.int16, 16, 128)
            values = [
                jnp.where(own, jnp.broadcast_to(term_ref[n, row, :], (16, 128)).astype(BF), BF(0))
                for n in range(3)
            ]
            left.append(jnp.concatenate(values, 0))
        return total + lax.dot_general(
            jnp.concatenate(left, 1), jnp.concatenate(right, 1), NT, preferred_element_type=F32
        )

    with jax.named_scope("gsum"):
        total = lax.fori_loop(0, 128 // SUM_ROWS, sum_step, jnp.zeros((48, 128), F32))
        pay_ref[...] = total[0:16] + total[16:32] + total[32:48]
    own_size_ref[...] = size_ref[...].astype(F32)

    with jax.named_scope("bar"):
        pl.semaphore_wait(barrier, NY + NZ + NF - 3)

    def hot_step(t, _):
        lanes = pl.ds(pl.multiple_of(256 * t, 256), 256)
        for f in range(32):
            wide = jnp.broadcast_to(bins_ref[f : f + 1, lanes], (BINS, 256)).astype(jnp.int8)
            hot_ref[BINS * f : BINS * (f + 1), lanes] = jnp.where(
                wide == iota0(jnp.int8, BINS, 256), F8(1), F8(0)
            )
        return 0

    def build(first, last):
        with jax.named_scope("build"):
            lax.fori_loop(first, last, hot_step, 0)

    def left_rows(parts):
        def step(t, _):
            for u in range(16):
                row = pl.ds(16 * t + u, 1)
                wide = jnp.broadcast_to(ids_ref[4, row, :], (LEAVES, 128)).astype(jnp.int8)
                member = wide == iota0(jnp.int8, LEAVES, 128)
                at = pl.ds(pl.multiple_of(2048 * t + 128 * u, 128), 128)
                for c in parts:
                    term = jnp.broadcast_to(term_ref[c, row, :], (LEAVES, 128)).astype(F8)
                    left_ref[LEAVES * c : LEAVES * (c + 1), at] = jnp.where(member, term, F8(0))
            return 0

        with jax.named_scope("left"):
            lax.fori_loop(0, 8, step, 0)

    def left_terms(c, value):
        first = value.astype(F8).astype(F32)
        term_ref[c] = first
        term_ref[c + 1] = ((value - first) * 16.0).astype(F8).astype(F32)

    for k in range(1, NY):
        send(pay_ref, pay_in.at[k - 1], pay_sems, y_peer(k)).start()
    for k in range(1, NY):
        send(own_size_ref, size_in_y.at[k - 1], size_sems, y_peer(k)).start()
    def low_hot_step(t, _):
        for u in range(4):
            wide = jnp.broadcast_to(ids_ref[2, pl.ds(4 * t + u, 1), :], (256, 128))
            at = pl.ds(pl.multiple_of(512 * t + 128 * u, 128), 128)
            low_hot_ref[:, at] = jnp.where(
                wide.astype(jnp.int16) == iota0(jnp.int16, 256, 128), BF(1), BF(0)
            )
        return 0

    with jax.named_scope("lowhot"):
        lax.fori_loop(0, 32, low_hot_step, 0)
    hess = h_ref[...].astype(F32)
    left_terms(2, hess * 128.0)
    left_rows((2, 3))
    with jax.named_scope("fetch"):
        fetch.wait()
    build(0, PARTS[0])
    with jax.named_scope("cwait"):
        wait_both(pay_in, pay_sems)
    mid_ref[...] = pay_ref[...] + pay_in[0] + pay_in[1] + pay_in[2]

    for k in range(1, NZ):
        send(mid_ref, mid_in.at[k - 1], mid_sems, z_peer(k)).start()
    wait_both(size_in_y, size_sems)
    size_z_ref[pl.ds(pl.multiple_of(4 * y, 4), 4), :] = own_size_ref[...]
    for k in range(1, NY):
        at = pl.ds(pl.multiple_of(4 * lax.rem(y + NY - k, NY), 4), 4)
        size_z_ref[at, :] = size_in_y[k - 1]

    @pl.when(z == feat)
    def _():
        for k in range(1, NZ):
            send(size_z_ref, size_in_ref, far_sems, z_peer(k)).start()

    build(PARTS[0], PARTS[1])

    with jax.named_scope("cwait"):
        wait_both(mid_in, mid_sems)

    @pl.when(z == feat)
    def _():
        wait(mid_in, far_sems[0])
        size_in_ref[...] = size_z_ref[...]

    @pl.when(z != feat)
    def _():
        wait(size_in_ref, far_sems[1])

    total = mid_ref[...]
    for k in range(NZ - 1):
        total = total + mid_in[k]
    mine = pl.ds(pl.multiple_of(16 * feat, 16), 16)
    table_ref[mine, :] = -total / (size_in_ref[...] + ratio_ref[0])

    for k in range(1, NF):
        send(table_ref.at[mine], table_ref.at[mine], table_sems, f_peer(k)).start()
    build(PARTS[1], PARTS[2])
    with jax.named_scope("cwait"):
        wait_both(table_ref.at[pl.ds(0, 16 * (NF - 1))], table_sems)

    table = table_ref[...]
    put_means = pltpu.make_async_copy(
        table_ref.at[pl.ds(pl.multiple_of(4 * rows, 4), 4)], mean_ref, mean_sem
    )
    put_means.start()
    wide = jnp.concatenate([table[0:64], table[64:128]], 1)
    wide = jnp.concatenate(split(wide, 2), 0).astype(BF)
    def look_step(block, _):
        span = 16384 // BLOCKS
        lanes = pl.ds(pl.multiple_of(span * block, span), span)
        found = jnp.dot(wide, low_hot_ref[:, lanes], preferred_element_type=F32)
        for u in range(span // 128):
            row = pl.ds(block * (span // 128) + u, 1)
            at = slice(128 * u, 128 * u + 128)
            part = found[0:64, at] + found[64:128, at]
            own = jnp.broadcast_to(ids_ref[3, row, :], (64, 128)) == iota0(I32, 64, 128)
            row_mean_ref[row, :] = jnp.sum(jnp.where(own, part, 0.0), axis=0, keepdims=True)
        return 0

    with jax.named_scope("look"):
        lax.fori_loop(0, BLOCKS, look_step, 0)
    bound = jnp.max(jnp.max(jnp.abs(table), axis=0, keepdims=True), axis=1, keepdims=True) + 6.0
    left_over = bound * 2.0**60
    scale = jnp.full_like(bound, 2.0**60)
    for step in (64, 32, 16, 8, 4, 2, 1):
        large = left_over >= 2.0**step
        left_over = jnp.where(large, left_over * 2.0**-step, left_over)
        scale = jnp.where(large, scale * 2.0**-step, scale)
    back = jnp.full_like(scale, 2.0**-7) / scale
    scale = scale * 2.0**7
    adjusted = (g_ref[...] + hess * row_mean_ref[...]).astype(BF).astype(F32)
    left_terms(0, adjusted * scale)
    left_rows((0, 1))

    low_half = lax.broadcasted_iota(I32, (8, 128), 1) < BINS

    def histogram(c):
        with jax.named_scope("mm"):
            hot = hot_ref[pl.ds(pl.multiple_of(512 * c, 512), 512), :]
            both = lax.dot_general(left_ref[...], hot, NT, preferred_element_type=F32)
            grad = (both[0:32] + both[32:64] * 0.0625) * back
            hess = (both[64:96] + both[96:128] * 0.0625) * (1.0 / 128.0)
            for to in range(NY):
                for pair in range(4):
                    a = grad[8 * to : 8 * to + 8, 128 * pair : 128 * pair + 128]
                    b = hess[8 * to : 8 * to + 8, 128 * pair : 128 * pair + 128]
                    out_y[c, to, 2 * pair] = jnp.where(low_half, a, pltpu.roll(b, 64, 1))
                    out_y[c, to, 2 * pair + 1] = jnp.where(low_half, pltpu.roll(a, 64, 1), b)

    def second_stage(c):
        with jax.named_scope("ywait"):
            wait_both(in_y.at[c], (y_send.at[c], y_recv.at[c]))
        for f in range(8):
            part = out_y[c, y, f] + in_y[c, 0, f] + in_y[c, 1, f] + in_y[c, 2, f]
            out_z[c, pl.ds(f, 8, stride=8), :] = part
        lines = pl.ds(pl.multiple_of(8 * c, 8), 8)
        for k in range(1, NZ):
            at = pl.ds(pl.multiple_of(8 * lax.rem(z + k, NZ), 8), 8)
            send(
                out_z.at[c, at], parts_ref.at[k - 1, lines], (z_send.at[c], z_recv.at[c]), z_peer(k)
            ).start()
        at = pl.ds(pl.multiple_of(8 * z, 8), 8)
        pltpu.make_async_copy(out_z.at[c, at], parts_ref.at[NZ - 1, lines], own_sem).start()

    def chunk(c, _):
        histogram(c)
        for k in range(1, NY):
            send(
                out_y.at[c, lax.rem(y + k, NY)], in_y.at[c, k - 1],
                (y_send.at[c], y_recv.at[c]), y_peer(k),
            ).start()

        @pl.when(c >= 2)
        def _():
            second_stage(c - 2)

        return 0

    lax.fori_loop(0, CHUNKS, chunk, 0)
    for c in (CHUNKS - 2, CHUNKS - 1):
        second_stage(c)
    with jax.named_scope("zwait"):
        for c in range(CHUNKS):
            wait_both(parts_ref.at[pl.ds(0, NZ - 1), pl.ds(8 * c, 8)], (z_send.at[c], z_recv.at[c]))
        wait(parts_ref.at[NZ - 1], own_sem)
    put_means.wait()


def last_sum(parts_ref, mean_ref, hist_ref, out_ref):
    total = parts_ref[0]
    for k in range(1, NZ):
        total = total + parts_ref[k]
    hist_ref[...] = total
    out_ref[...] = mean_ref[...]


def shards(gradient, hessian, groups, leaf_ids, bins, group_sizes, variance_ratio):
    count = gradient.shape[0]
    vmem, sem = pltpu.VMEM, pltpu.SemaphoreType.DMA
    whole = pl.BlockSpec(memory_space=pltpu.VMEM)
    parts, means = pl.pallas_call(
        kernel,
        out_shape=(jax.ShapeDtypeStruct((NZ, 32, 128), F32), jax.ShapeDtypeStruct((4, 128), F32)),
        in_specs=[whole] * 5
        + [pl.BlockSpec(memory_space=pltpu.SMEM), pl.BlockSpec(memory_space=pl.ANY)],
        out_specs=(pl.BlockSpec(memory_space=pl.ANY),) * 2,
        scratch_shapes=[
            vmem((32, count), I32),
            vmem((32 * BINS, count), F8),
            vmem((4 * LEAVES, count), F8),
            vmem((256, count), BF),
            vmem((5, 128, 128), I32),
            vmem((4, 128, 128), F32),
            vmem((128, 128), F32),
            vmem((16, 128), F32),
            vmem((NY - 1, 16, 128), F32),
            vmem((16, 128), F32),
            vmem((NZ - 1, 16, 128), F32),
            vmem((4, 128), F32),
            vmem((NY - 1, 4, 128), F32),
            vmem((16, 128), F32),
            vmem((16, 128), F32),
            vmem((128, 128), F32),
            vmem((CHUNKS, NY, 8, 8, 128), F32),
            vmem((CHUNKS, NY - 1, 8, 8, 128), F32),
            vmem((CHUNKS, 64, 128), F32),
            sem, sem, sem,
            sem((5,)), sem((5,)),
            sem((CHUNKS,)), sem((CHUNKS,)), sem((CHUNKS,)), sem((CHUNKS,)),
        ],
        compiler_params=pltpu.CompilerParams(
            collective_id=0, has_side_effects=True, vmem_limit_bytes=56 * 1024 * 1024
        ),
    )(
        gradient.reshape(128, 128),
        hessian.reshape(128, 128),
        groups.reshape(128, 128),
        leaf_ids.reshape(128, 128),
        group_sizes.reshape(4, 128),
        variance_ratio,
        bins,
    )
    hist, means = pl.pallas_call(
        last_sum,
        out_shape=(jax.ShapeDtypeStruct((32, 128), F32), jax.ShapeDtypeStruct((4, 128), F32)),
        in_specs=[whole] * 2,
        out_specs=(whole, whole),
    )(parts, means)
    return hist.reshape(1, 32, 128), means.reshape(512)


def solution(mesh):
    in_specs = (P("rows"), P("rows"), P("rows"), P("rows"), P("feat", "rows"), P("rows"), P())
    out_specs = (P("rows", "feat", None), P("rows"))
    return jax.shard_map(shards, mesh=mesh, in_specs=in_specs, out_specs=out_specs, check_vma=False)
```

time: 49.2 us -> 45.5 us (0.925)
  local copies, waits for them, and re-layouts: 2.55 us -> 0 us
  Pallas kernels: 45.1 us -> 44.1 us
    unnamed x2 -> x0, local copies, waits for them, and re-layouts: 2.55 us -> none
    pallas_call x1 -> x2, Pallas kernels: 45.1 us -> 44.1 us  [the longest x1 42.6 us: shards(): pl.pallas_call(kernel, out_shape=(jax.ShapeDtypeStruct((NZ, 32, 128), F32...]
where the time goes in v3:
time: 45.5 us; the launch traced here: 45.4 us
  Pallas kernels  44.1 us (97%)
  between operations  1.29 us (3%)
    pallas_call x1, Pallas kernels, shards(): pl.pallas_call(kernel, out_shape=(jax.ShapeDtypeStruct((NZ, 32, 128), F32...  42.6 us
    pallas_call x1, Pallas kernels, shards(): pl.pallas_call(last_sum, out_shape=(jax.ShapeDtypeStruct((32, 128), F32),...  1.53 us

profile of v3, /device:TPU:1, one launch (start us, length us, event | category | flops | bytes accessed | tf_op | source)
XLA Modules:
  0.0 45.4 jit_solution(8844982876030117281)
XLA Ops:
  1.3 42.6 %shard_map.86 = (f32[8,32,128]{2,1,0:T(8,128)}, f32[4,128]{1,0:T(4,128)}) custom-call(f32[128,128]{1,0:T(8,128)} %bitcast.7, bf16[128,128]{1,0:T(8,128)(2,1)} %bitcast.10, s32[128,128]{1,0:T(8,128)} %bitcast.8, s32[128,128]{1,0:T(8,128)} %bitcast.9, s32[4,128]{1,0:T(4,128)} %bitcast.11, f32[1]{0:T(128)S(6)} %copy.9.ratio_ref, s32[32,16384]{1,0:T(8,128)} %bins_hbm.1), custom_call_target="tpu_custom_call" | custom-call | tf_op jit(solution)/shard_map/pallas_call | solution.py:319
  43.9 1.5 %shard_map.87 = (f32[32,128]{1,0:T(8,128)}, f32[4,128]{1,0:T(4,128)}) custom-call(f32[8,32,128]{2,1,0:T(8,128)} %get-tuple-element.6.parts_ref, f32[4,128]{1,0:T(4,128)} %get-tuple-element.7.mean_ref), custom_call_target="tpu_custom_call" | custom-call | tf_op jit(solution)/shard_map/pallas_call | solution.py:361

commit v4 on v3

--- a/solution.py
+++ b/solution.py
@@ -19,7 +19,9 @@
 BLOCKS = 2
 SUM_ROWS = 64
 CHUNKS = 4
-PARTS = (4, 46, 64)
+PARTS = (44, 64)
+LOW_PART = 24
+FAR_Y, FAR_Z, FAR_F = (2, 1, 3), (4, 3, 5, 2, 6, 1, 7), (4, 5, 3, 2, 6, 7, 1)
 
 
 def iota0(dtype, rows, lanes):
@@ -36,13 +38,13 @@
 
 
 def kernel(
-    g_ref, h_ref, group_ref, leaf_ref, size_ref, ratio_ref, bins_hbm,
+    g_hbm, h_hbm, group_hbm, leaf_hbm, size_hbm, ratio_ref, bins_hbm,
     parts_ref, mean_ref,
-    bins_ref, hot_ref, left_ref, low_hot_ref,
+    g_ref, h_ref, group_ref, leaf_ref, size_ref, bins_ref, hot_ref, left_ref, low_hot_ref,
     ids_ref, term_ref, row_mean_ref,
     pay_ref, pay_in, mid_ref, mid_in, own_size_ref, size_in_y, size_z_ref, size_in_ref, table_ref,
     out_y, in_y, out_z,
-    bins_sem, mean_sem, own_sem, send_sem, recv_sem, y_send, y_recv, z_send, z_recv,
+    in_sem, mean_sem, own_sem, send_sem, recv_sem, y_send, y_recv, z_send, z_recv,
 ):
     rows, feat = lax.axis_index("rows"), lax.axis_index("feat")
     z, y = rows // NY, lax.rem(rows, NY)
@@ -80,8 +82,24 @@
         + [f_peer(k) for k in range(1, NF)]
     ):
         pl.semaphore_signal(barrier, inc=1, device_id=peer, device_id_type=MESH)
-    fetch = pltpu.make_async_copy(bins_hbm, bins_ref, bins_sem)
-    fetch.start()
+    fetches = [
+        pltpu.make_async_copy(src, dst, in_sem.at[n])
+        for n, (src, dst) in enumerate(
+            (
+                (group_hbm, group_ref),
+                (g_hbm, g_ref),
+                (leaf_hbm, leaf_ref),
+                (h_hbm, h_ref),
+                (size_hbm, size_ref),
+                (bins_hbm, bins_ref),
+            )
+        )
+    ]
+    for fetch in fetches:
+        fetch.start()
+    with jax.named_scope("fetch"):
+        for fetch in fetches[:5]:
+            fetch.wait()
 
     ids = group_ref[...]
     high, low = lax.shift_right_logical(ids, 7), ids & 127
@@ -152,9 +170,9 @@
         term_ref[c] = first
         term_ref[c + 1] = ((value - first) * 16.0).astype(F8).astype(F32)
 
-    for k in range(1, NY):
+    for k in FAR_Y:
         send(pay_ref, pay_in.at[k - 1], pay_sems, y_peer(k)).start()
-    for k in range(1, NY):
+    for k in FAR_Y:
         send(own_size_ref, size_in_y.at[k - 1], size_sems, y_peer(k)).start()
     def low_hot_step(t, _):
         for u in range(4):
@@ -166,18 +184,15 @@
         return 0
 
     with jax.named_scope("lowhot"):
-        lax.fori_loop(0, 32, low_hot_step, 0)
+        lax.fori_loop(0, LOW_PART, low_hot_step, 0)
     hess = h_ref[...].astype(F32)
     left_terms(2, hess * 128.0)
     left_rows((2, 3))
-    with jax.named_scope("fetch"):
-        fetch.wait()
-    build(0, PARTS[0])
     with jax.named_scope("cwait"):
         wait_both(pay_in, pay_sems)
     mid_ref[...] = pay_ref[...] + pay_in[0] + pay_in[1] + pay_in[2]
 
-    for k in range(1, NZ):
+    for k in FAR_Z:
         send(mid_ref, mid_in.at[k - 1], mid_sems, z_peer(k)).start()
     wait_both(size_in_y, size_sems)
     size_z_ref[pl.ds(pl.multiple_of(4 * y, 4), 4), :] = own_size_ref[...]
@@ -187,10 +202,11 @@
 
     @pl.when(z == feat)
     def _():
-        for k in range(1, NZ):
+        for k in FAR_Z:
             send(size_z_ref, size_in_ref, far_sems, z_peer(k)).start()
 
-    build(PARTS[0], PARTS[1])
+    fetches[5].wait()
+    build(0, PARTS[0])
 
     with jax.named_scope("cwait"):
         wait_both(mid_in, mid_sems)
@@ -210,9 +226,11 @@
     mine = pl.ds(pl.multiple_of(16 * feat, 16), 16)
     table_ref[mine, :] = -total / (size_in_ref[...] + ratio_ref[0])
 
-    for k in range(1, NF):
+    for k in FAR_F:
         send(table_ref.at[mine], table_ref.at[mine], table_sems, f_peer(k)).start()
-    build(PARTS[1], PARTS[2])
+    with jax.named_scope("lowhot"):
+        lax.fori_loop(LOW_PART, 32, low_hot_step, 0)
+    build(PARTS[0], PARTS[1])
     with jax.named_scope("cwait"):
         wait_both(table_ref.at[pl.ds(0, 16 * (NF - 1))], table_sems)
 
@@ -272,7 +290,7 @@
             part = out_y[c, y, f] + in_y[c, 0, f] + in_y[c, 1, f] + in_y[c, 2, f]
             out_z[c, pl.ds(f, 8, stride=8), :] = part
         lines = pl.ds(pl.multiple_of(8 * c, 8), 8)
-        for k in range(1, NZ):
+        for k in FAR_Z:
             at = pl.ds(pl.multiple_of(8 * lax.rem(z + k, NZ), 8), 8)
             send(
                 out_z.at[c, at], parts_ref.at[k - 1, lines], (z_send.at[c], z_recv.at[c]), z_peer(k)
@@ -282,7 +300,7 @@
 
     def chunk(c, _):
         histogram(c)
-        for k in range(1, NY):
+        for k in FAR_Y:
             send(
                 out_y.at[c, lax.rem(y + k, NY)], in_y.at[c, k - 1],
                 (y_send.at[c], y_recv.at[c]), y_peer(k),
@@ -319,10 +337,15 @@
     parts, means = pl.pallas_call(
         kernel,
         out_shape=(jax.ShapeDtypeStruct((NZ, 32, 128), F32), jax.ShapeDtypeStruct((4, 128), F32)),
-        in_specs=[whole] * 5
+        in_specs=[pl.BlockSpec(memory_space=pl.ANY)] * 5
         + [pl.BlockSpec(memory_space=pltpu.SMEM), pl.BlockSpec(memory_space=pl.ANY)],
         out_specs=(pl.BlockSpec(memory_space=pl.ANY),) * 2,
         scratch_shapes=[
+            vmem((128, 128), F32),
+            vmem((128, 128), BF),
+            vmem((128, 128), I32),
+            vmem((128, 128), I32),
+            vmem((4, 128), I32),
             vmem((32, count), I32),
             vmem((32 * BINS, count), F8),
             vmem((4 * LEAVES, count), F8),
@@ -342,7 +365,7 @@
             vmem((CHUNKS, NY, 8, 8, 128), F32),
             vmem((CHUNKS, NY - 1, 8, 8, 128), F32),
             vmem((CHUNKS, 64, 128), F32),
-            sem, sem, sem,
+            sem((6,)), sem, sem,
             sem((5,)), sem((5,)),
             sem((CHUNKS,)), sem((CHUNKS,)), sem((CHUNKS,)), sem((CHUNKS,)),
         ],

time: 45.5 us -> 43.5 us (0.956)
  Pallas kernels: 44.1 us -> 42 us
    pallas_call x1, Pallas kernels: 42.6 us -> 40.5 us  [shards(): pl.pallas_call(kernel, out_shape=(jax.ShapeDtypeStruct((NZ, 32, 128), F32...]
where the time goes in v4:
time: 43.5 us; the launch traced here: 43.3 us
  Pallas kernels  42 us (97%)
  between operations  1.29 us (3%)
    pallas_call x1, Pallas kernels, shards(): pl.pallas_call(kernel, out_shape=(jax.ShapeDtypeStruct((NZ, 32, 128), F32...  40.5 us
    pallas_call x1, Pallas kernels, shards(): pl.pallas_call(last_sum, out_shape=(jax.ShapeDtypeStruct((32, 128), F32),...  1.53 us

profile of v4, /device:TPU:1, one launch (start us, length us, event | category | flops | bytes accessed | tf_op | source)
XLA Modules:
  0.0 43.3 jit_solution(16341317714249171435)
XLA Ops:
  1.3 40.5 %shard_map.86 = (f32[8,32,128]{2,1,0:T(8,128)}, f32[4,128]{1,0:T(4,128)}) custom-call(f32[128,128]{1,0:T(8,128)} %bitcast.7, bf16[128,128]{1,0:T(8,128)(2,1)} %bitcast.10, s32[128,128]{1,0:T(8,128)} %bitcast.8, s32[128,128]{1,0:T(8,128)} %bitcast.9, s32[4,128]{1,0:T(4,128)} %bitcast.11, f32[1]{0:T(128)S(6)} %copy.9.ratio_ref, s32[32,16384]{1,0:T(8,128)} %bins_hbm.1), custom_call_target="tpu_custom_call" | custom-call | tf_op jit(solution)/shard_map/pallas_call | solution.py:337
  41.8 1.5 %shard_map.87 = (f32[32,128]{1,0:T(8,128)}, f32[4,128]{1,0:T(4,128)}) custom-call(f32[8,32,128]{2,1,0:T(8,128)} %get-tuple-element.6.parts_ref, f32[4,128]{1,0:T(4,128)} %get-tuple-element.7.mean_ref), custom_call_target="tpu_custom_call" | custom-call | tf_op jit(solution)/shard_map/pallas_call | solution.py:384

commit v5 on v4

--- a/solution.py
+++ b/solution.py
@@ -19,9 +19,9 @@
 BLOCKS = 2
 SUM_ROWS = 64
 CHUNKS = 4
-PARTS = (44, 64)
-LOW_PART = 24
-FAR_Y, FAR_Z, FAR_F = (2, 1, 3), (4, 3, 5, 2, 6, 1, 7), (4, 5, 3, 2, 6, 7, 1)
+LOW_FIRST, BUILD_FIRST = (32, 16), (54, 44)
+FAR_Y, FAR_Z = (2, 1, 3), (4, 3, 5, 2, 6, 1, 7)
+FAR_F = ((2, 0), (1, 0), (3, 0), (2, 1), (1, 1), (3, 1), (0, 0))
 
 
 def iota0(dtype, rows, lanes):
@@ -48,6 +48,7 @@
 ):
     rows, feat = lax.axis_index("rows"), lax.axis_index("feat")
     z, y = rows // NY, lax.rem(rows, NY)
+    x, core = feat // 2, lax.rem(feat, 2)
 
     def y_peer(k):
         return (z * NY + lax.rem(y + k, NY), feat)
@@ -103,7 +104,7 @@
 
     ids = group_ref[...]
     high, low = lax.shift_right_logical(ids, 7), ids & 127
-    ids_ref[0] = high - 16 * feat
+    ids_ref[0] = high - 32 * x
     ids_ref[1] = low
     ids_ref[2] = low + 2 * (high & 64)
     ids_ref[3] = high & 63
@@ -118,10 +119,10 @@
             row = pl.ds(SUM_ROWS * n + t, 1)
             wide = jnp.broadcast_to(ids_ref[1, row, :], (128, 128)).astype(jnp.int16)
             right.append(jnp.where(wide == iota0(jnp.int16, 128, 128), BF(1), BF(0)))
-            wide = jnp.broadcast_to(ids_ref[0, row, :], (16, 128)).astype(jnp.int16)
-            own = wide == iota0(jnp.int16, 16, 128)
+            wide = jnp.broadcast_to(ids_ref[0, row, :], (32, 128)).astype(jnp.int16)
+            own = wide == iota0(jnp.int16, 32, 128)
             values = [
-                jnp.where(own, jnp.broadcast_to(term_ref[n, row, :], (16, 128)).astype(BF), BF(0))
+                jnp.where(own, jnp.broadcast_to(term_ref[n, row, :], (32, 128)).astype(BF), BF(0))
                 for n in range(3)
             ]
             left.append(jnp.concatenate(values, 0))
@@ -129,9 +130,12 @@
             jnp.concatenate(left, 1), jnp.concatenate(right, 1), NT, preferred_element_type=F32
         )
 
-    with jax.named_scope("gsum"):
-        total = lax.fori_loop(0, 128 // SUM_ROWS, sum_step, jnp.zeros((48, 128), F32))
-        pay_ref[...] = total[0:16] + total[16:32] + total[32:48]
+    @pl.when(core == 1)
+    def _():
+        with jax.named_scope("gsum"):
+            total = lax.fori_loop(0, 128 // SUM_ROWS, sum_step, jnp.zeros((96, 128), F32))
+            pay_ref[...] = total[0:32] + total[32:64] + total[64:96]
+
     own_size_ref[...] = size_ref[...].astype(F32)
 
     with jax.named_scope("bar"):
@@ -170,10 +174,16 @@
         term_ref[c] = first
         term_ref[c + 1] = ((value - first) * 16.0).astype(F8).astype(F32)
 
-    for k in FAR_Y:
-        send(pay_ref, pay_in.at[k - 1], pay_sems, y_peer(k)).start()
-    for k in FAR_Y:
-        send(own_size_ref, size_in_y.at[k - 1], size_sems, y_peer(k)).start()
+    @pl.when(core == 1)
+    def _():
+        for k in FAR_Y:
+            send(pay_ref, pay_in.at[k - 1], pay_sems, y_peer(k)).start()
+        for k in FAR_Y:
+            send(own_size_ref, size_in_y.at[k - 1], size_sems, y_peer(k)).start()
+
+    low_first = jnp.where(core == 1, LOW_FIRST[1], LOW_FIRST[0])
+    build_first = jnp.where(core == 1, BUILD_FIRST[1], BUILD_FIRST[0])
+
     def low_hot_step(t, _):
         for u in range(4):
             wide = jnp.broadcast_to(ids_ref[2, pl.ds(4 * t + u, 1), :], (256, 128))
@@ -184,55 +194,75 @@
         return 0
 
     with jax.named_scope("lowhot"):
-        lax.fori_loop(0, LOW_PART, low_hot_step, 0)
+        lax.fori_loop(0, low_first, low_hot_step, 0)
     hess = h_ref[...].astype(F32)
     left_terms(2, hess * 128.0)
     left_rows((2, 3))
+    @pl.when(core == 1)
+    def _():
+        with jax.named_scope("cwait"):
+            wait_both(pay_in, pay_sems)
+        mid_ref[...] = pay_ref[...] + pay_in[0] + pay_in[1] + pay_in[2]
+        for k in FAR_Z:
+            send(mid_ref, mid_in.at[k - 1], mid_sems, z_peer(k)).start()
+        wait_both(size_in_y, size_sems)
+        size_z_ref[pl.ds(pl.multiple_of(4 * y, 4), 4), :] = own_size_ref[...]
+        for k in range(1, NY):
+            at = pl.ds(pl.multiple_of(4 * lax.rem(y + NY - k, NY), 4), 4)
+            size_z_ref[at, :] = size_in_y[k - 1]
+
+    has_sizes = (core == 1) & (z // 2 == x)
+    size_rows = pl.ds(pl.multiple_of(16 * lax.rem(z, 2), 16), 16)
+
+    @pl.when(has_sizes)
+    def _():
+        for k in FAR_Z:
+            send(size_z_ref, size_in_ref.at[size_rows], far_sems, z_peer(k)).start()
+
+    fetches[5].wait()
+    build(0, build_first)
+
+    @pl.when(core == 1)
+    def _():
+        with jax.named_scope("cwait"):
+            wait_both(mid_in, mid_sems)
+
+    @pl.when(has_sizes)
+    def _():
+        wait(mid_in.at[:, pl.ds(0, 16)], far_sems[0])
+        wait(size_z_ref, far_sems[1])
+        size_in_ref[size_rows, :] = size_z_ref[...]
+
+    @pl.when((core == 1) & (z // 2 != x))
+    def _():
+        wait(size_in_ref, far_sems[1])
+
+    mine = pl.ds(pl.multiple_of(32 * x, 32), 32)
+
+    @pl.when(core == 1)
+    def _():
+        total = mid_ref[...]
+        for k in range(NZ - 1):
+            total = total + mid_in[k]
+        table_ref[mine, :] = -total / (size_in_ref[...] + ratio_ref[0])
+        for k, to in FAR_F:
+            peer = (rows, 2 * lax.rem(x + k, 4) + to)
+            send(table_ref.at[mine], table_ref.at[mine], table_sems, peer).start()
+
+    with jax.named_scope("lowhot"):
+        lax.fori_loop(low_first, 32, low_hot_step, 0)
+    build(build_first, 64)
+
     with jax.named_scope("cwait"):
-        wait_both(pay_in, pay_sems)
-    mid_ref[...] = pay_ref[...] + pay_in[0] + pay_in[1] + pay_in[2]
-
-    for k in FAR_Z:
-        send(mid_ref, mid_in.at[k - 1], mid_sems, z_peer(k)).start()
-    wait_both(size_in_y, size_sems)
-    size_z_ref[pl.ds(pl.multiple_of(4 * y, 4), 4), :] = own_size_ref[...]
-    for k in range(1, NY):
-        at = pl.ds(pl.multiple_of(4 * lax.rem(y + NY - k, NY), 4), 4)
-        size_z_ref[at, :] = size_in_y[k - 1]
-
-    @pl.when(z == feat)
-    def _():
-        for k in FAR_Z:
-            send(size_z_ref, size_in_ref, far_sems, z_peer(k)).start()
-
-    fetches[5].wait()
-    build(0, PARTS[0])
-
-    with jax.named_scope("cwait"):
-        wait_both(mid_in, mid_sems)
-
-    @pl.when(z == feat)
-    def _():
-        wait(mid_in, far_sems[0])
-        size_in_ref[...] = size_z_ref[...]
-
-    @pl.when(z != feat)
-    def _():
-        wait(size_in_ref, far_sems[1])
-
-    total = mid_ref[...]
-    for k in range(NZ - 1):
-        total = total + mid_in[k]
-    mine = pl.ds(pl.multiple_of(16 * feat, 16), 16)
-    table_ref[mine, :] = -total / (size_in_ref[...] + ratio_ref[0])
-
-    for k in FAR_F:
-        send(table_ref.at[mine], table_ref.at[mine], table_sems, f_peer(k)).start()
-    with jax.named_scope("lowhot"):
-        lax.fori_loop(LOW_PART, 32, low_hot_step, 0)
-    build(PARTS[0], PARTS[1])
-    with jax.named_scope("cwait"):
-        wait_both(table_ref.at[pl.ds(0, 16 * (NF - 1))], table_sems)
+
+        @pl.when(core == 1)
+        def _():
+            wait(mid_in, table_sems[0])
+            wait(table_ref.at[pl.ds(0, 96)], table_sems[1])
+
+        @pl.when(core == 0)
+        def _():
+            wait(table_ref, table_sems[1])
 
     table = table_ref[...]
     put_means = pltpu.make_async_copy(
@@ -270,18 +300,26 @@
 
     low_half = lax.broadcasted_iota(I32, (8, 128), 1) < BINS
 
-    def histogram(c):
+    def histogram(c, first, count):
         with jax.named_scope("mm"):
-            hot = hot_ref[pl.ds(pl.multiple_of(512 * c, 512), 512), :]
+            start = pl.multiple_of(512 * c + BINS * first, BINS * count)
+            hot = hot_ref[pl.ds(start, BINS * count), :]
             both = lax.dot_general(left_ref[...], hot, NT, preferred_element_type=F32)
             grad = (both[0:32] + both[32:64] * 0.0625) * back
             hess = (both[64:96] + both[96:128] * 0.0625) * (1.0 / 128.0)
             for to in range(NY):
-                for pair in range(4):
+                for pair in range(count // 2):
                     a = grad[8 * to : 8 * to + 8, 128 * pair : 128 * pair + 128]
                     b = hess[8 * to : 8 * to + 8, 128 * pair : 128 * pair + 128]
-                    out_y[c, to, 2 * pair] = jnp.where(low_half, a, pltpu.roll(b, 64, 1))
-                    out_y[c, to, 2 * pair + 1] = jnp.where(low_half, pltpu.roll(a, 64, 1), b)
+                    f = first + 2 * pair
+                    out_y[c, to, f] = jnp.where(low_half, a, pltpu.roll(b, 64, 1))
+                    out_y[c, to, f + 1] = jnp.where(low_half, pltpu.roll(a, 64, 1), b)
+        at = pl.ds(first, count)
+        for k in FAR_Y:
+            send(
+                out_y.at[c, lax.rem(y + k, NY), at], in_y.at[c, k - 1, at],
+                (y_send.at[c], y_recv.at[c]), y_peer(k),
+            ).start()
 
     def second_stage(c):
         with jax.named_scope("ywait"):
@@ -299,12 +337,7 @@
         pltpu.make_async_copy(out_z.at[c, at], parts_ref.at[NZ - 1, lines], own_sem).start()
 
     def chunk(c, _):
-        histogram(c)
-        for k in FAR_Y:
-            send(
-                out_y.at[c, lax.rem(y + k, NY)], in_y.at[c, k - 1],
-                (y_send.at[c], y_recv.at[c]), y_peer(k),
-            ).start()
+        histogram(c, 0, 8)
 
         @pl.when(c >= 2)
         def _():
@@ -312,9 +345,14 @@
 
         return 0
 
-    lax.fori_loop(0, CHUNKS, chunk, 0)
-    for c in (CHUNKS - 2, CHUNKS - 1):
-        second_stage(c)
+    def last_chunk(n, _):
+        histogram(CHUNKS - 1, 4 * n, 4)
+        second_stage(CHUNKS - 3 + n)
+        return 0
+
+    lax.fori_loop(0, CHUNKS - 1, chunk, 0)
+    lax.fori_loop(0, 2, last_chunk, 0)
+    second_stage(CHUNKS - 1)
     with jax.named_scope("zwait"):
         for c in range(CHUNKS):
             wait_both(parts_ref.at[pl.ds(0, NZ - 1), pl.ds(8 * c, 8)], (z_send.at[c], z_recv.at[c]))
@@ -353,14 +391,14 @@
             vmem((5, 128, 128), I32),
             vmem((4, 128, 128), F32),
             vmem((128, 128), F32),
-            vmem((16, 128), F32),
-            vmem((NY - 1, 16, 128), F32),
-            vmem((16, 128), F32),
-            vmem((NZ - 1, 16, 128), F32),
+            vmem((32, 128), F32),
+            vmem((NY - 1, 32, 128), F32),
+            vmem((32, 128), F32),
+            vmem((NZ - 1, 32, 128), F32),
             vmem((4, 128), F32),
             vmem((NY - 1, 4, 128), F32),
             vmem((16, 128), F32),
-            vmem((16, 128), F32),
+            vmem((32, 128), F32),
             vmem((128, 128), F32),
             vmem((CHUNKS, NY, 8, 8, 128), F32),
             vmem((CHUNKS, NY - 1, 8, 8, 128), F32),

time: 43.5 us -> 41.5 us (0.954)
  Pallas kernels: 42 us -> 40.1 us
    pallas_call x1, Pallas kernels: 40.5 us -> 38.5 us  [shards(): pl.pallas_call(kernel, out_shape=(jax.ShapeDtypeStruct((NZ, 32, 128), F32...]
where the time goes in v5:
time: 41.5 us; the launch traced here: 41.4 us
  Pallas kernels  40.1 us (97%)
  between operations  1.29 us (3%)
    pallas_call x1, Pallas kernels, shards(): pl.pallas_call(kernel, out_shape=(jax.ShapeDtypeStruct((NZ, 32, 128), F32...  38.5 us
    pallas_call x1, Pallas kernels, shards(): pl.pallas_call(last_sum, out_shape=(jax.ShapeDtypeStruct((32, 128), F32),...  1.53 us

profile of v5, /device:TPU:1, one launch (start us, length us, event | category | flops | bytes accessed | tf_op | source)
XLA Modules:
  0.0 41.4 jit_solution(15235357905061858074)
XLA Ops:
  1.3 38.5 %shard_map.86 = (f32[8,32,128]{2,1,0:T(8,128)}, f32[4,128]{1,0:T(4,128)}) custom-call(f32[128,128]{1,0:T(8,128)} %bitcast.7, bf16[128,128]{1,0:T(8,128)(2,1)} %bitcast.10, s32[128,128]{1,0:T(8,128)} %bitcast.8, s32[128,128]{1,0:T(8,128)} %bitcast.9, s32[4,128]{1,0:T(4,128)} %bitcast.11, f32[1]{0:T(128)S(6)} %copy.9.ratio_ref, s32[32,16384]{1,0:T(8,128)} %bins_hbm.1), custom_call_target="tpu_custom_call" | custom-call | tf_op jit(solution)/shard_map/pallas_call | solution.py:375
  39.8 1.5 %shard_map.87 = (f32[32,128]{1,0:T(8,128)}, f32[4,128]{1,0:T(4,128)}) custom-call(f32[8,32,128]{2,1,0:T(8,128)} %get-tuple-element.6.parts_ref, f32[4,128]{1,0:T(4,128)} %get-tuple-element.7.mean_ref), custom_call_target="tpu_custom_call" | custom-call | tf_op jit(solution)/shard_map/pallas_call | solution.py:422

commit v6 on v5

--- a/solution.py
+++ b/solution.py
@@ -15,7 +15,7 @@
 I32 = jnp.int32
 MESH = pl.DeviceIdType.MESH
 NT = (((1,), (1,)), ((), ()))
-NY, NZ, NF = 4, 8, 8
+NY, NZ = 4, 8
 BLOCKS = 2
 SUM_ROWS = 64
 CHUNKS = 4
@@ -56,9 +56,6 @@
     def z_peer(k):
         return (lax.rem(z + k, NZ) * NY + y, feat)
 
-    def f_peer(k):
-        return (rows, lax.rem(feat + k, NF))
-
     def send(src, dst, sems, peer):
         return pltpu.make_async_remote_copy(
             src_ref=src, dst_ref=dst, send_sem=sems[0], recv_sem=sems[1],
@@ -77,12 +74,18 @@
     ]
 
     barrier = pltpu.get_barrier_semaphore()
-    for peer in (
-        [y_peer(k) for k in range(1, NY)]
-        + [z_peer(k) for k in range(1, NZ)]
-        + [f_peer(k) for k in range(1, NF)]
-    ):
-        pl.semaphore_signal(barrier, inc=1, device_id=peer, device_id_type=MESH)
+
+    def tell(*peers):
+        for peer in peers:
+            pl.semaphore_signal(barrier, inc=1, device_id=peer, device_id_type=MESH)
+
+    tell(*[z_peer(k) for k in FAR_Z], *[y_peer(k) for k in FAR_Y])
+    tell(*[(rows, 2 * lax.rem(x + k, 4) + 1) for k in (2, 1, 3)])
+
+    @pl.when(core == 0)
+    def _():
+        tell((rows, feat + 1))
+
     fetches = [
         pltpu.make_async_copy(src, dst, in_sem.at[n])
         for n, (src, dst) in enumerate(
@@ -139,7 +142,7 @@
     own_size_ref[...] = size_ref[...].astype(F32)
 
     with jax.named_scope("bar"):
-        pl.semaphore_wait(barrier, NY + NZ + NF - 3)
+        pl.semaphore_wait(barrier, 10 + 7 * core)
 
     def hot_step(t, _):
         lanes = pl.ds(pl.multiple_of(256 * t, 256), 256)

time: 41.5 us -> 41.5 us (level)
  no operation moved by 1% of the time
where the time goes in v6:
time: 41.5 us; the launch traced here: 41.4 us
  Pallas kernels  40.1 us (97%)
  between operations  1.29 us (3%)
    pallas_call x1, Pallas kernels, shards(): pl.pallas_call(kernel, out_shape=(jax.ShapeDtypeStruct((NZ, 32, 128), F32...  38.6 us
    pallas_call x1, Pallas kernels, shards(): pl.pallas_call(last_sum, out_shape=(jax.ShapeDtypeStruct((32, 128), F32),...  1.53 us

profile of v6, /device:TPU:1, one launch (start us, length us, event | category | flops | bytes accessed | tf_op | source)
XLA Modules:
  0.0 41.4 jit_solution(1005991737480439898)
XLA Ops:
  1.3 38.6 %shard_map.86 = (f32[8,32,128]{2,1,0:T(8,128)}, f32[4,128]{1,0:T(4,128)}) custom-call(f32[128,128]{1,0:T(8,128)} %bitcast.7, bf16[128,128]{1,0:T(8,128)(2,1)} %bitcast.10, s32[128,128]{1,0:T(8,128)} %bitcast.8, s32[128,128]{1,0:T(8,128)} %bitcast.9, s32[4,128]{1,0:T(4,128)} %bitcast.11, f32[1]{0:T(128)S(6)} %copy.9.ratio_ref, s32[32,16384]{1,0:T(8,128)} %bins_hbm.1), custom_call_target="tpu_custom_call" | custom-call | tf_op jit(solution)/shard_map/pallas_call | solution.py:378
  39.9 1.5 %shard_map.87 = (f32[32,128]{1,0:T(8,128)}, f32[4,128]{1,0:T(4,128)}) custom-call(f32[8,32,128]{2,1,0:T(8,128)} %get-tuple-element.6.parts_ref, f32[4,128]{1,0:T(4,128)} %get-tuple-element.7.mean_ref), custom_call_target="tpu_custom_call" | custom-call | tf_op jit(solution)/shard_map/pallas_call | solution.py:425
